TPU v7x, 128 devices: a whole 4x4x4 slice. The times are simulated.
128 devices in a mesh: req: 32 (over z, x, core), tp: 4 (over y).
Axes of the slice: x: 4, y: 4, z: 4, core: 2. Of those that a mesh axis runs over, the one named last changes fastest.
Arguments:
- tokens: bfloat16 [16384, 2560], P('req'), may hold values from -6 to 6
- lengths: int32 [32], P('req'), may hold values from 1 to 512, as said below
- page_slot: int32 [128], replicated, may hold values from 0 to 127, as said below
- trainer_layout: int32 [128], replicated, may hold values from 0 to 127, each once
- trainer_qkv: float32 [2560, 3840], P(('req', 'tp'))
- trainer_gateup: float32 [2560, 13824], P(('req', 'tp')), may hold values from -0.125 to 0.125
- attn_gain: float32 [2560], replicated, may hold values from 0.1 to 1.9
- ffn_gain: float32 [2560], replicated, may hold values from 0.1 to 1.9
- out_proj: bfloat16 [2560, 2560], P('tp'), may hold values from -0.125 to 0.125
- down_proj: bfloat16 [6912, 2560], P('tp'), may hold values from -0.078125 to 0.078125
Outputs:
- layer_out: bfloat16 [16384, 2560], P(('req', 'tp'))
- kv_cache: bfloat16 [128, 128, 1280], P('req', None, 'tp')
Inputs may be any that keep to these rules, and one draw needn't show every extreme that they name: `lengths`: heavy-tailed; some request has exactly 512. `page_slot`: a permutation; pool slot s belongs to request device s // 4; the 4 pages of one request belong to 4 different devices. `trainer_layout`: a permutation; shard s is the trainer shard on the device with index s over req and tp together.
All inputs are finite; a program needn't handle non-finite values.
Results may differ from a plain program's by a relative error of at most 0.0065.
The roundings to bfloat16 on the way count: a program that leaves them out, or rounds other values in their place, can miss the bound.
Values may be sent and summed in bfloat16 or wider, within the bound.
A program may use at most 192 MiB of HBM per device.

v0:
```python
import jax
import jax.numpy as jnp
from jax import lax
from jax.sharding import PartitionSpec as P

HD = 80
PAGE = 128


eps_norm = 1e-05
theta_base = 10000.0


def normed(values, gain):
    scale = lax.rsqrt(jnp.mean(values * values, axis=-1, keepdims=True) + eps_norm)
    return (values * scale * gain).astype(jnp.bfloat16)


def rotary(field, head_dim):
    half = head_dim // 2
    count = field.shape[0]
    freq = theta_base ** (-jnp.arange(half, dtype=jnp.float32) * 2.0 / head_dim)
    angles = jnp.arange(count, dtype=jnp.float32)[:, None] * freq[None, :]
    cosine = jnp.cos(angles)[:, None, :]
    sine = jnp.sin(angles)[:, None, :]
    first = field[..., :half]
    second = field[..., half:]
    return jnp.concatenate(
        [first * cosine - second * sine, second * cosine + first * sine], axis=-1
    )


def body(
    tokens,
    lengths,
    page_slot,
    trainer_layout,
    trainer_qkv,
    trainer_gateup,
    attn_gain,
    ffn_gain,
    out_proj,
    down_proj,
):
    n_tp = lax.axis_size("tp")
    n_req = lax.axis_size("req")
    devices = n_tp * n_req
    rows_each = trainer_qkv.shape[0]
    seq_len = tokens.shape[0]
    model_dim = tokens.shape[1]
    head_dim = HD
    local_heads = out_proj.shape[0] // head_dim
    group_cols = trainer_qkv.shape[1] // n_tp
    local_kv = (group_cols // head_dim - local_heads) // 2
    group = local_heads // local_kv
    q_cols = local_heads * head_dim
    k_cols = local_kv * head_dim
    ff_local = down_proj.shape[0]
    qkv_half, gu_half = (
        lax.all_to_all(
            trainer_qkv.astype(jnp.bfloat16), "tp", split_axis=1, concat_axis=0, tiled=True
        ),
        lax.all_to_all(
            trainer_gateup.astype(jnp.bfloat16), "tp", split_axis=1, concat_axis=0, tiled=True
        ),
    )
    x_f = tokens.astype(jnp.float32)
    x_norm = normed(x_f, attn_gain)
    inverse = (
        jnp.zeros((devices,), jnp.int32)
        .at[trainer_layout]
        .set(jnp.arange(devices, dtype=jnp.int32))
    )
    qkv_all, gu_all = (
        lax.all_gather(qkv_half, "req", axis=0, tiled=True),
        lax.all_gather(gu_half, "req", axis=0, tiled=True),
    )
    qkv_weight = qkv_all.reshape(devices, rows_each, qkv_all.shape[1])[inverse].reshape(
        model_dim, qkv_all.shape[1]
    )
    gu_weight = gu_all.reshape(devices, rows_each, gu_all.shape[1])[inverse].reshape(
        model_dim, gu_all.shape[1]
    )
    joined = jnp.dot(x_norm, qkv_weight, preferred_element_type=jnp.float32)
    query = rotary(joined[:, :q_cols].reshape(seq_len, local_heads, head_dim), head_dim)
    keys = rotary(
        joined[:, q_cols : q_cols + k_cols].reshape(seq_len, local_kv, head_dim), head_dim
    )
    query16 = query.astype(jnp.bfloat16).reshape(seq_len, local_kv, group, head_dim)
    keys16 = keys.astype(jnp.bfloat16)
    values16 = (
        joined[:, q_cols + k_cols :].reshape(seq_len, local_kv, head_dim).astype(jnp.bfloat16)
    )
    scores = jnp.einsum(
        "qkgd,skd->kgqs", query16, keys16, preferred_element_type=jnp.float32
    ) * head_dim ** (-0.5)
    slots = jnp.arange(seq_len, dtype=jnp.int32)
    length = lengths[0]
    allowed = (slots[None, :] <= slots[:, None]) & (slots[None, :] < length)
    scores = jnp.where(allowed[None, None], scores, -1e30)
    probs = jax.nn.softmax(scores, axis=-1).astype(jnp.bfloat16)
    context = jnp.einsum(
        "kgqs,skd->qkgd", probs, values16, preferred_element_type=jnp.float32
    ).astype(jnp.bfloat16)
    partial_out = jnp.dot(
        context.reshape(seq_len, q_cols), out_proj, preferred_element_type=jnp.float32
    )
    share = seq_len // n_tp
    tp_index = lax.axis_index("tp")
    mixed = lax.psum(partial_out, "tp")
    resid = x_f + mixed
    h_norm = normed(resid, ffn_gain)
    resid_share = lax.dynamic_slice_in_dim(resid, tp_index * share, share, 0)
    projected = jnp.dot(h_norm, gu_weight, preferred_element_type=jnp.float32)
    hidden = (jax.nn.silu(projected[:, :ff_local]) * projected[:, ff_local:]).astype(jnp.bfloat16)
    down = jnp.dot(hidden, down_proj, preferred_element_type=jnp.float32)
    added = lax.psum_scatter(down, "tp", scatter_dimension=0, tiled=True)
    share_slots = tp_index * share + jnp.arange(share, dtype=jnp.int32)
    live_share = (share_slots < length).astype(jnp.float32)
    layer_out = ((resid_share + added) * live_share[:, None]).astype(jnp.bfloat16)
    live_rows = (slots < length)[:, None]
    key_rows = keys16.reshape(seq_len, k_cols)
    value_rows = values16.reshape(seq_len, k_cols)
    cache_rows = jnp.concatenate(
        [
            jnp.where(live_rows, key_rows, jnp.zeros_like(key_rows)),
            jnp.where(live_rows, value_rows, jnp.zeros_like(value_rows)),
        ],
        axis=1,
    )
    pages = cache_rows.reshape(seq_len // PAGE, PAGE, 2 * k_cols)
    pool_size = pages.shape[0]
    owner = lax.axis_index("req")
    targets = owner * pool_size + jnp.arange(pool_size, dtype=jnp.int32)
    picks = (page_slot[:, None] == targets[None, :]).astype(jnp.bfloat16)
    pool = jnp.einsum(
        "np,nsc->psc",
        picks,
        lax.all_gather(pages, "req", axis=0, tiled=True),
        preferred_element_type=jnp.float32,
    )
    kv_cache = pool.astype(jnp.bfloat16)
    return (layer_out, kv_cache)


def solution(mesh):
    return jax.shard_map(
        body,
        mesh=mesh,
        in_specs=(
            P("req", None),
            P("req"),
            P(),
            P(),
            P(("req", "tp"), None),
            P(("req", "tp"), None),
            P(),
            P(),
            P("tp", None),
            P("tp", None),
        ),
        out_specs=(P(("req", "tp"), None), P("req", None, "tp")),
        check_vma=False,
    )
```

profile of v0, /device:TPU:1, one launch (start us, length us, event | category | flops | bytes accessed | tf_op | source)
XLA Modules:
  0.0 472.2 jit_solution(814724774709201183)
XLA Ops:
  10.3 10.0 %all_to_all.38 = bf16[20,4,960]{2,0,1:T(8,128)(2,1)S(1)} all-to-all(bf16[20,4,960]{2,0,1:T(8,128)(2,1)S(1)} %copy.18), channel_id=1, replica_groups=mesh['req'=32,'tp'=4] {'tp'}, dimensions={1} | all-to-all | bytes 307200 | tf_op jit(solution)/shard_map/all_to_all | solution.py:60
  23.4 2.3 fusion.4
  27.0 43.9 %all-gather.4.cloned.1.call-done = bf16[2560,960]{1,0:T(8,128)(2,1)} async-done(((bf16[80,960]{1,0:T(8,128)(2,1)}), bf16[2560,960]{1,0:T(8,128)(2,1)}) %all-gather.4.cloned.1.call-update) | async-done | bytes 4915216 | tf_op jit(solution)/shard_map/all_gather | solution.py:75
  70.9 9.7 %reshape.159 = bf16[128,20,960]{2,1,0:T(8,128)(2,1)} reshape(bf16[2560,960]{1,0:T(8,128)(2,1)} %all-gather.4.cloned.1.call-done) | data formatting | bytes 9830400 | tf_op jit(solution)/shard_map/reshape | solution.py:78
  80.6 6.4 %gather_fusion = bf16[128,20,960]{2,1,0:T(8,128)(2,1)} fusion(bf16[128,20,960]{2,1,0:T(8,128)(2,1)} %reshape.159, s32[1024]{0:T(1024)S(1)} %pad_clamp_fusion), kind=kCustom, calls=%fused_computation | custom fusion | bytes 9830912 | tf_op jit(solution)/shard_map/gather | solution.py:78
  87.0 9.8 %reshape.160 = bf16[2560,960]{1,0:T(8,128)(2,1)} reshape(bf16[128,20,960]{2,1,0:T(8,128)(2,1)} %gather_fusion) | data formatting | bytes 9830400 | tf_op jit(solution)/shard_map/reshape | solution.py:78
  96.8 6.2 %fusion.13 = f32[512,960]{0,1:T(8,128)S(1)} fusion(bf16[2560,960]{1,0:T(8,128)(2,1)} %reshape.160, bf16[512,2560]{1,0:T(8,128)(2,1)} %param.10, f32[2560]{0:T(1024)S(1)} %copy-done.7, f32[512]{0:T(512)S(1)} %add_rsqrt_fusion.1), kind=kOutput, calls=%fused_computation.25 | convolution fusion | flops 2521825280 | bytes 9515008 | tf_op jit(solution)/shard_map/dot_general | solution.py:84
  105.6 7.6 %fusion.49 = (f32[2,4,512]{2,1,0:T(4,128)S(1)}, f32[2,4,512,512]{2,3,1,0:T(8,128)}) fusion(pred[512,512]{0,1:T(8,128)(4,1)} %fusion.26, bf16[512,2,4,40]{0,3,2,1:T(8,128)(2,1)} %bitcast.65, bf16[512,2,4,40]{0,3,2,1:T(8,128)(2,1)} %bitcast.64, bf16[512,2,40]{0,2,1:T(8,128)(2,1)} %get-tuple-element.15, bf16[512,2,40]{0,2,1:T(8,128)(2,1)S(1)} %get-tuple-element.14), kind=kOutput, calls=%fused_computation.76 | convolution fusion | flops 345571840 | bytes 9486336 | tf_op jit(solution)/shard_map/sub | solution.py:101
  113.2 4.2 fusion.22
  117.4 4.6 fusion.54
  122.1 2.4 convert_element_type.68
  125.9 21.6 %all_to_all.39 = bf16[20,4,3456]{2,0,1:T(8,128)(2,1)} all-to-all(bf16[20,4,3456]{2,0,1:T(8,128)(2,1)S(1)} %copy.20), channel_id=1, replica_groups=mesh['req'=32,'tp'=4] {'tp'}, dimensions={1} | all-to-all | bytes 1105920 | tf_op jit(solution)/shard_map/all_to_all | solution.py:63
  147.5 2.0 all_to_all.35
  150.8 86.5 %all-reduce.2.cloned.1.call-done = f32[512,2560]{1,0:T(8,128)} async-done(((f32[512,2560]{1,0:T(8,128)}), f32[512,2560]{1,0:T(8,128)}) %all-reduce.2.cloned.1.call-update) | async-done | bytes 5242896 | tf_op jit(solution)/shard_map/psum | solution.py:110
  237.4 5.4 %multiply_reduce_fusion = (f32[512]{0:T(512)S(1)}, f32[512,2560]{1,0:T(8,128)}) fusion(f32[512,2560]{1,0:T(8,128)} %all-reduce.2.cloned.1.call-done, bf16[512,2560]{1,0:T(8,128)(2,1)S(1)} %copy-done.2), kind=kLoop, calls=%fused_computation.17 | loop fusion | flops 5242368 | bytes 13109248 | tf_op jit(solution)/shard_map/reduce_sum | solution.py:15
  242.8 72.6 %all-gather.6.cloned.1.call-done = bf16[2560,3456]{1,0:T(8,128)(2,1)} async-done(((bf16[80,3456]{1,0:T(8,128)(2,1)}), bf16[2560,3456]{1,0:T(8,128)(2,1)}) %all-gather.6.cloned.1.call-update) | async-done | bytes 17694736 | tf_op jit(solution)/shard_map/all_gather | solution.py:76
  315.4 24.5 %reshape.164 = bf16[128,20,3456]{2,1,0:T(8,128)(2,1)} reshape(bf16[2560,3456]{1,0:T(8,128)(2,1)} %all-gather.6.cloned.1.call-done) | data formatting | bytes 35389440 | tf_op jit(solution)/shard_map/reshape | solution.py:81
  339.9 17.0 %gather_fusion.1 = bf16[128,20,3456]{2,1,0:T(8,128)(2,1)} fusion(bf16[128,20,3456]{2,1,0:T(8,128)(2,1)} %reshape.164, s32[1024]{0:T(1024)S(1)} %pad_clamp_fusion), kind=kCustom, calls=%fused_computation.1 | custom fusion | bytes 35389952 | tf_op jit(solution)/shard_map/gather | solution.py:81
  356.9 25.1 %reshape.165 = bf16[2560,3456]{1,0:T(8,128)(2,1)} reshape(bf16[128,20,3456]{2,1,0:T(8,128)(2,1)} %gather_fusion.1) | data formatting | bytes 35389440 | tf_op jit(solution)/shard_map/reshape | solution.py:81
  382.0 15.3 %fusion.12 = f32[512,3456]{1,0:T(8,128)S(1)} fusion(bf16[2560,3456]{1,0:T(8,128)(2,1)} %reshape.165, f32[512,2560]{1,0:T(8,128)} %get-tuple-element.11, f32[2560]{0:T(1024)S(1)} %copy-done.8, f32[512]{0:T(512)S(1)} %add_rsqrt_fusion), kind=kOutput, calls=%fused_computation.24 | convolution fusion | flops 9063628800 | bytes 30027776 | tf_op jit(solution)/shard_map/dot_general | solution.py:114
  397.3 10.4 %fusion.19 = f32[512,2560]{1,0:T(8,128)} fusion(bf16[1728,2560]{1,0:T(8,128)(2,1)} %param.19, f32[512,3456]{1,0:T(8,128)S(1)} %fusion.12), kind=kOutput, calls=%fused_computation.30 | convolution fusion | flops 4535156736 | bytes 21430272 | tf_op jit(solution)/shard_map/dot_general | solution.py:116
  408.4 9.9 %fusion.23 = bf16[4,128,320]{1,0,2:T(4,128)(2,1)S(1)} fusion(bf16[128,128,320]{1,2,0:T(8,128)(2,1)} %all-gather.8.cloned.1.call-done, s32[128]{0:T(128)S(1)} %copy-done.6, s32[4]{0:T(128)S(1)} %iota_add_fusion), kind=kOutput, calls=%fused_computation.34 | convolution fusion | flops 42107392 | bytes 10813968 | tf_op jit(solution)/shard_map/np,nsc->psc/dot_general | solution.py:136
  419.1 43.9 %reduce-scatter.2.cloned.1.call-done = f32[128,2560]{1,0:T(8,128)} async-done(((f32[512,2560]{1,0:T(8,128)}), f32[128,2560]{1,0:T(8,128)}) %reduce-scatter.2.cloned.1.call-update) | async-done | bytes 1310736 | tf_op jit(solution)/shard_map/reduce_scatter | solution.py:117
  462.9 2.7 multiply_convert_fusion.2
  (60 shorter events, 13.4 us)
Async XLA Ops:
  7.2 110.3 %copy-start = (bf16[640,2560]{1,0:T(8,128)(2,1)S(1)}, bf16[640,2560]{1,0:T(8,128)(2,1)}, u32[]{:S(2)}) copy-start(bf16[640,2560]{1,0:T(8,128)(2,1)} %param.18) | copy-start | bytes 9830404
  7.2 63.7 %all-gather.4.cloned.1.call-start = ((), (), s32[]{:S(2)}) async-start(), calls=%async_computation.3 | async-start | bytes 5406720 | tf_op jit(solution)/shard_map/all_gather | solution.py:75
  21.0 216.3 %all-reduce.2.cloned.1.call-start = ((), (), s32[]{:S(2)}) async-start(), calls=%async_computation.4 | async-start | bytes 10485760 | tf_op jit(solution)/shard_map/psum | solution.py:110
  87.0 9.8 %copy-start.7 = (f32[2560]{0:T(1024)S(1)}, f32[2560]{0:T(1024)}, u32[]{:S(2)}) copy-start(f32[2560]{0:T(1024)} %param.16) | copy-start | bytes 30724
  105.6 7.6 %copy-start.5 = (bf16[512,160]{0,1:T(8,128)(2,1)S(1)}, bf16[512,160]{0,1:T(8,128)(2,1)}, u32[]{:S(2)}) copy-start(bf16[512,160]{0,1:T(8,128)(2,1)} %get-tuple-element.9) | copy-start | bytes 491524
  122.0 27.8 %copy-start.3 = (bf16[20,4,8,128]{3,2,1,0:T(8,128)(2,1)S(1)}, bf16[20,4,8,128]{3,2,1,0:T(8,128)(2,1)}, u32[]{:S(2)}) copy-start(bf16[20,4,8,128]{3,2,1,0:T(8,128)(2,1)} %get-tuple-element.8) | copy-start | bytes 491524
  122.0 27.8 %copy-start.4 = (bf16[512,2,40]{0,2,1:T(8,128)(2,1)S(1)}, bf16[512,2,40]{0,2,1:T(8,128)(2,1)}, u32[]{:S(2)}) copy-start(bf16[512,2,40]{0,2,1:T(8,128)(2,1)} %get-tuple-element.15) | copy-start | bytes 245764
  122.0 115.3 %copy-start.2 = (bf16[512,2560]{1,0:T(8,128)(2,1)S(1)}, bf16[512,2560]{1,0:T(8,128)(2,1)}, u32[]{:S(2)}) copy-start(bf16[512,2560]{1,0:T(8,128)(2,1)} %param.10) | copy-start | bytes 7864324
  122.1 193.3 %all-gather.6.cloned.1.call-start = ((), (), s32[]{:S(2)}) async-start(), calls=%async_computation.5 | async-start | bytes 18247680 | tf_op jit(solution)/shard_map/all_gather | solution.py:76
  149.6 258.2 %all-gather.8.cloned.1.call-start = ((), (), s32[]{:S(2)}) async-start(), calls=%async_computation.7 | async-start | bytes 10813440 | tf_op jit(solution)/shard_map/all_gather | solution.py:139
  150.8 312.2 %reduce-scatter.2.cloned.1.call-start = ((), (), s32[]{:S(2)}) async-start(), calls=%async_computation.6 | async-start | bytes 6553600 | tf_op jit(solution)/shard_map/reduce_scatter | solution.py:117
  356.9 25.1 %copy-start.8 = (f32[2560]{0:T(1024)S(1)}, f32[2560]{0:T(1024)}, u32[]{:S(2)}) copy-start(f32[2560]{0:T(1024)} %param.17) | copy-start | bytes 30724
  407.7 0.7 copy-start.6
  407.8 57.9 %copy-start.1 = (bf16[640,2560]{1,0:T(8,128)(2,1)S(1)}, bf16[640,2560]{1,0:T(8,128)(2,1)}, u32[]{:S(2)}) copy-start(bf16[640,2560]{1,0:T(8,128)(2,1)} %param.18) | copy-start | bytes 9830404
Sparse Core Ops, SparseCore 0:
  21.1 49.7 all-gather.3
  122.2 115.1 all-reduce.1
  240.3 75.0 all-gather.5
  318.1 57.3 all-gather.7
  407.9 55.0 reduce-scatter.1
where the time goes:
time: 474 us; the launch traced here: 472 us
  waiting for transfers between devices  247 us (52%)
  local copies, waits for them, and re-layouts  101 us (21%)
  matrix products  58.2 us (12%)
  blocking collectives  31.6 us (7%)
  other arithmetic  19.2 us (4%)
  between operations  14.6 us (3%)
    psum x1, waiting for transfers between devices, body(): mixed = lax.psum(partial_out, 'tp')  86.5 us
    all_gather x1, waiting for transfers between devices, body(): lax.all_gather(gu_half, 'req', axis=0, tiled=True)  72.6 us
    reshape x2, local copies, waits for them, and re-layouts, body(): gu_all.reshape(devices, rows_each, gu_all.shape[1])[inverse]  49.7 us
    all_gather x1, waiting for transfers between devices, body(): lax.all_gather(qkv_half, 'req', axis=0, tiled=True)  43.9 us
    reduce_scatter x1, waiting for transfers between devices, body(): added = lax.psum_scatter(down, 'tp', scatter_dimension=0, tiled=True)  43.9 us
    all_to_all x1, blocking collectives, body(): lax.all_to_all(trainer_gateup.astype(jnp.bfloat16), 'tp', split_axis=1, c...  21.6 us
    reshape x2, local copies, waits for them, and re-layouts, body(): qkv_all.reshape(devices, rows_each, qkv_all.shape[1])[inverse]  19.5 us
    gather x1, local copies, waits for them, and re-layouts, body(): gu_all.reshape(devices, rows_each, gu_all.shape[1])[inverse]  17 us
  transfers between devices with their start and end apart: 5, of which 4 were waited for; matrix products, arithmetic and copies ran while one was open for 25% of the time, Pallas kernels for 0%

commit v1 on v0

--- a/solution.py
+++ b/solution.py
@@ -66,21 +66,11 @@
     )
     x_f = tokens.astype(jnp.float32)
     x_norm = normed(x_f, attn_gain)
-    inverse = (
-        jnp.zeros((devices,), jnp.int32)
-        .at[trainer_layout]
-        .set(jnp.arange(devices, dtype=jnp.int32))
-    )
-    qkv_all, gu_all = (
-        lax.all_gather(qkv_half, "req", axis=0, tiled=True),
-        lax.all_gather(gu_half, "req", axis=0, tiled=True),
-    )
-    qkv_weight = qkv_all.reshape(devices, rows_each, qkv_all.shape[1])[inverse].reshape(
-        model_dim, qkv_all.shape[1]
-    )
-    gu_weight = gu_all.reshape(devices, rows_each, gu_all.shape[1])[inverse].reshape(
-        model_dim, gu_all.shape[1]
-    )
+    row_of = (trainer_layout[:, None] * rows_each + jnp.arange(rows_each, dtype=jnp.int32)).reshape(1, -1)
+    place = (jnp.arange(model_dim, dtype=jnp.int32)[:, None] == row_of).astype(jnp.bfloat16)
+    x_norm = jnp.dot(x_norm, place, preferred_element_type=jnp.float32).astype(jnp.bfloat16)
+    qkv_weight = lax.all_gather(qkv_half, "req", axis=0, tiled=True)
+    gu_weight = lax.all_gather(gu_half, "req", axis=0, tiled=True)
     joined = jnp.dot(x_norm, qkv_weight, preferred_element_type=jnp.float32)
     query = rotary(joined[:, :q_cols].reshape(seq_len, local_heads, head_dim), head_dim)
     keys = rotary(
@@ -107,14 +97,20 @@
     )
     share = seq_len // n_tp
     tp_index = lax.axis_index("tp")
-    mixed = lax.psum(partial_out, "tp")
-    resid = x_f + mixed
-    h_norm = normed(resid, ffn_gain)
-    resid_share = lax.dynamic_slice_in_dim(resid, tp_index * share, share, 0)
+    mixed = lax.psum_scatter(
+        partial_out.astype(jnp.bfloat16), "tp", scatter_dimension=0, tiled=True
+    )
+    x_share = lax.dynamic_slice_in_dim(tokens, tp_index * share, share, 0)
+    resid_share = x_share.astype(jnp.float32) + mixed.astype(jnp.float32)
+    h_share = normed(resid_share, ffn_gain)
+    h_share = jnp.dot(h_share, place, preferred_element_type=jnp.float32).astype(jnp.bfloat16)
+    h_norm = lax.all_gather(h_share, "tp", axis=0, tiled=True)
     projected = jnp.dot(h_norm, gu_weight, preferred_element_type=jnp.float32)
     hidden = (jax.nn.silu(projected[:, :ff_local]) * projected[:, ff_local:]).astype(jnp.bfloat16)
     down = jnp.dot(hidden, down_proj, preferred_element_type=jnp.float32)
-    added = lax.psum_scatter(down, "tp", scatter_dimension=0, tiled=True)
+    added = lax.psum_scatter(
+        down.astype(jnp.bfloat16), "tp", scatter_dimension=0, tiled=True
+    ).astype(jnp.float32)
     share_slots = tp_index * share + jnp.arange(share, dtype=jnp.int32)
     live_share = (share_slots < length).astype(jnp.float32)
     layer_out = ((resid_share + added) * live_share[:, None]).astype(jnp.bfloat16)

time: 474 us -> 365 us (0.77)
  local copies, waits for them, and re-layouts: 101 us -> 4.84 us
  matrix products: 58.2 us -> 72.3 us
  waiting for transfers between devices: 247 us -> 236 us
  blocking collectives: 31.6 us -> 22.4 us
  other arithmetic: 19.2 us -> 14.1 us
    psum x1 -> x0, waiting for transfers between devices: 86.5 us -> none  [body(): mixed = lax.psum(partial_out, 'tp')]
    reshape x4 -> x0, local copies, waits for them, and re-layouts: 69.2 us -> none  [the longest x2 49.7 us: body(): gu_all.reshape(devices, rows_each, gu_all.shape[1])[inverse]]
    all_gather x1, waiting for transfers between devices: 0.02 us -> 35.4 us  [body(): lax.all_gather(pages, 'req', axis=0, tiled=True)]
    all_gather x2 -> x3, waiting for transfers between devices: 117 us -> 142 us  [the longest x1 76.9 us: body(): gu_weight = lax.all_gather(gu_half, 'req', axis=0, tiled=True)]
    gather x2 -> x0, local copies, waits for them, and re-layouts: 23.4 us -> none  [the longest x1 17 us: body(): gu_all.reshape(devices, rows_each, gu_all.shape[1])[inverse]]
    reduce_scatter x1 -> x2, waiting for transfers between devices: 43.9 us -> 57.9 us  [the longest x1 33 us: body(): lax.psum_scatter(partial_out.astype(jnp.bfloat16), 'tp', scatter_dimensio...]
    all_to_all x1, blocking collectives: 21.6 us -> 12.4 us  [body(): lax.all_to_all(trainer_gateup.astype(jnp.bfloat16), 'tp', split_axis=1, c...]
    dot_general x1, matrix products: 6.15 us -> 14.3 us  [body(): joined = jnp.dot(x_norm, qkv_weight, preferred_element_type=jnp.float32)]
  transfers between devices with their start and end apart: 5 -> 6, of which waited for: 4 -> 6; matrix products, arithmetic and copies ran while one was open for 25% -> 11% of each run, Pallas kernels for 0% -> 0%
where the time goes in v1:
time: 365 us
  waiting for transfers between devices  236 us (65%)
  matrix products  72.3 us (20%)
  blocking collectives  22.4 us (6%)
  between operations  15 us (4%)
  other arithmetic  14.1 us (4%)
  local copies, waits for them, and re-layouts  4.84 us (1%)
    all_gather x1, waiting for transfers between devices, body(): gu_weight = lax.all_gather(gu_half, 'req', axis=0, tiled=True)  76.9 us
    all_gather x1, waiting for transfers between devices, body(): qkv_weight = lax.all_gather(qkv_half, 'req', axis=0, tiled=True)  44.8 us
    all_gather x1, waiting for transfers between devices, body(): lax.all_gather(pages, 'req', axis=0, tiled=True)  35.4 us
    reduce_scatter x1, waiting for transfers between devices, body(): lax.psum_scatter(partial_out.astype(jnp.bfloat16), 'tp', scatter_dimensio...  33 us
    reduce_scatter x1, waiting for transfers between devices, body(): lax.psum_scatter(down.astype(jnp.bfloat16), 'tp', scatter_dimension=0, ti...  24.9 us
    all_gather x1, waiting for transfers between devices, body(): h_norm = lax.all_gather(h_share, 'tp', axis=0, tiled=True)  20.4 us
    dot_general x1, matrix products, body(): projected = jnp.dot(h_norm, gu_weight, preferred_element_type=jnp.float32)  14.5 us
    dot_general x1, matrix products, body(): joined = jnp.dot(x_norm, qkv_weight, preferred_element_type=jnp.float32)  14.3 us
  transfers between devices with their start and end apart: 6, of which 6 were waited for; matrix products, arithmetic and copies ran while one was open for 11% of the time, Pallas kernels for 0%

profile of v1, /device:TPU:1, one launch (start us, length us, event | category | flops | bytes accessed | tf_op | source)
XLA Modules:
  0.0 364.6 jit_solution(9727156666313900420)
XLA Ops:
  7.2 1.2 convert_element_type.84
  8.4 0.9 all_to_all.28
  9.3 1.0 copy.18
  10.3 10.0 %all_to_all.38 = bf16[20,4,960]{2,0,1:T(8,128)(2,1)S(1)} all-to-all(bf16[20,4,960]{2,0,1:T(8,128)(2,1)S(1)} %copy.18), channel_id=1, replica_groups=mesh['req'=32,'tp'=4] {'tp'}, dimensions={1} | all-to-all | bytes 307200 | tf_op jit(solution)/shard_map/all_to_all | solution.py:60
  22.6 2.3 fusion.8
  26.2 44.8 %all-gather.5.cloned.1.call-done = bf16[2560,960]{1,0:T(8,128)(2,1)} async-done(((bf16[80,960]{1,0:T(8,128)(2,1)}), bf16[2560,960]{1,0:T(8,128)(2,1)}) %all-gather.5.cloned.1.call-update) | async-done | bytes 4915216 | tf_op jit(solution)/shard_map/all_gather | solution.py:72
  70.9 14.3 %fusion.57 = f32[512,960]{0,1:T(8,128)} fusion(bf16[2560,960]{1,0:T(8,128)(2,1)} %all-gather.5.cloned.1.call-done, s32[2560]{0:T(1024)S(1)} %add.92, bf16[512,2560]{1,0:T(8,128)(2,1)} %param.10, f32[2560]{0:T(1024)S(1)} %copy-done.7, f32[512]{0:T(512)S(1)} %add_rsqrt_fusion), kind=kOutput, calls=%fused_computation.79 | convolution fusion | flops 9240576000 | bytes 9525248 | tf_op jit(solution)/shard_map/dot_general | solution.py:74
  85.2 1.8 select_bitcast_fusion
  87.1 1.0 subtract_convert_fusion
  88.8 7.8 %fusion.52 = (f32[2,4,512]{2,1,0:T(4,128)S(1)}, f32[2,4,512,512]{2,3,1,0:T(8,128)}) fusion(pred[512,512]{0,1:T(8,128)(4,1)} %fusion.27, bf16[512,2,4,40]{0,3,2,1:T(8,128)(2,1)} %bitcast.67, bf16[512,2,4,40]{0,3,2,1:T(8,128)(2,1)} %bitcast.66, bf16[512,2,40]{0,2,1:T(8,128)(2,1)} %get-tuple-element.13, bf16[512,2,40]{0,2,1:T(8,128)(2,1)S(1)} %get-tuple-element.12), kind=kOutput, calls=%fused_computation.78 | convolution fusion | flops 345571840 | bytes 9486336 | tf_op jit(solution)/shard_map/sub | solution.py:91
  96.6 4.2 %fusion.23 = bf16[2,80,4,512]{3,1,2,0:T(8,128)(2,1)S(1)} fusion(bf16[512,2,80,1]{0,2,3,1:T(8,128)(2,1)S(1)} %bitcast.68, f32[2,4,512,512]{2,3,1,0:T(8,128)} %get-tuple-element.17, f32[2,4,512]{2,1,0:T(4,128)S(1)} %get-tuple-element.16), kind=kOutput, calls=%fused_computation.30 | convolution fusion | flops 340066304 | bytes 9224192 | tf_op jit(solution)/shard_map/kgqs,skd->qkgd/dot_general | solution.py:92
  100.8 3.8 %convolution_convert_fusion.1 = bf16[512,2560]{1,0:T(8,128)(2,1)} fusion(bf16[512,640]{0,1:T(8,128)(2,1)S(1)} %bitcast.64, bf16[640,2560]{1,0:T(8,128)(2,1)S(1)} %copy-done), kind=kOutput, calls=%fused_computation.19 | convolution fusion | flops 1679032320 | bytes 6553600 | tf_op jit(solution)/shard_map/dot_general | solution.py:95
  104.7 33.0 %reduce-scatter.3.cloned.1.call-done = bf16[128,2560]{1,0:T(8,128)(2,1)} async-done(((bf16[512,2560]{1,0:T(8,128)(2,1)}), bf16[128,2560]{1,0:T(8,128)(2,1)}) %reduce-scatter.3.cloned.1.call-update) | async-done | bytes 655376 | tf_op jit(solution)/shard_map/reduce_scatter | solution.py:100
  137.7 1.6 multiply_reduce_fusion
  139.3 8.0 %fusion.17 = bf16[128,2560]{1,0:T(8,128)(2,1)} fusion(s32[2560]{0:T(1024)S(1)} %add.92, bf16[128,2560]{1,0:T(8,128)(2,1)} %reduce-scatter.3.cloned.1.call-done, f32[2560]{0:T(1024)S(1)} %copy-done.8, f32[128]{0:T(128)S(1)} %add_rsqrt_fusion.1, bf16[512,2560]{1,0:T(8,128)(2,1)} %param.10, s32[]{:T(128)S(6)} %select_n.15), kind=kOutput, calls=%fused_computation.26 | convolution fusion | flops 1686568960 | bytes 1987076 | tf_op jit(solution)/shard_map/dot_general | solution.py:106
  147.8 12.4 %all_to_all.39 = bf16[20,4,3456]{2,0,1:T(8,128)(2,1)S(1)} all-to-all(bf16[20,4,3456]{2,0,1:T(8,128)(2,1)S(1)} %copy.20), channel_id=1, replica_groups=mesh['req'=32,'tp'=4] {'tp'}, dimensions={1} | all-to-all | bytes 1105920 | tf_op jit(solution)/shard_map/all_to_all | solution.py:63
  162.4 20.4 %all-gather.7.cloned.1.call-done = bf16[512,2560]{1,0:T(8,128)(2,1)} async-done(((bf16[128,2560]{1,0:T(8,128)(2,1)}), bf16[512,2560]{1,0:T(8,128)(2,1)}) %all-gather.7.cloned.1.call-update) | async-done | bytes 2621456 | tf_op jit(solution)/shard_map/all_gather | solution.py:107
  182.9 76.9 %all-gather.9.cloned.1.call-done = bf16[2560,3456]{1,0:T(8,128)(2,1)} async-done(((bf16[80,3456]{1,0:T(8,128)(2,1)}), bf16[2560,3456]{1,0:T(8,128)(2,1)}) %all-gather.9.cloned.1.call-update) | async-done | bytes 17694736 | tf_op jit(solution)/shard_map/all_gather | solution.py:73
  259.8 14.5 %fusion.58 = f32[512,3456]{1,0:T(8,128)S(1)} fusion(bf16[512,2560]{1,0:T(8,128)(2,1)} %all-gather.7.cloned.1.call-done, bf16[2560,3456]{1,0:T(8,128)(2,1)} %all-gather.9.cloned.1.call-done), kind=kOutput, calls=%fused_computation.80 | convolution fusion | flops 9059696640 | bytes 27394048 | tf_op jit(solution)/shard_map/dot_general | solution.py:108
  274.3 10.0 %convolution_convert_fusion = bf16[512,2560]{1,0:T(8,128)(2,1)} fusion(bf16[1728,2560]{1,0:T(8,128)(2,1)} %param.19, f32[512,3456]{1,0:T(8,128)S(1)} %fusion.58), kind=kOutput, calls=%fused_computation.18 | convolution fusion | flops 4536467456 | bytes 18808832 | tf_op jit(solution)/shard_map/dot_general | solution.py:110
  284.4 35.4 %all-gather.11.cloned.1.call-done = bf16[128,128,320]{1,2,0:T(8,128)(2,1)} async-done(((bf16[4,128,320]{1,2,0:T(8,128)(2,1)}), bf16[128,128,320]{1,2,0:T(8,128)(2,1)}) %all-gather.11.cloned.1.call-update) | async-done | bytes 10485776 | tf_op jit(solution)/shard_map/all_gather | solution.py:135
  319.8 9.8 %fusion.24 = bf16[4,128,320]{1,0,2:T(4,128)(2,1)S(1)} fusion(bf16[128,128,320]{1,2,0:T(8,128)(2,1)} %all-gather.11.cloned.1.call-done, s32[128]{0:T(128)S(1)} %copy-done.6, s32[4]{0:T(128)S(1)} %iota_add_fusion.1), kind=kOutput, calls=%fused_computation.35 | convolution fusion | flops 42107392 | bytes 10813968 | tf_op jit(solution)/shard_map/np,nsc->psc/dot_general | solution.py:132
  330.3 24.9 %reduce-scatter.5.cloned.1.call-done = bf16[128,2560]{1,0:T(8,128)(2,1)} async-done(((bf16[512,2560]{1,0:T(8,128)(2,1)}), bf16[128,2560]{1,0:T(8,128)(2,1)}) %reduce-scatter.5.cloned.1.call-update) | async-done | bytes 655376 | tf_op jit(solution)/shard_map/reduce_scatter | solution.py:111
  355.2 2.6 multiply_convert_fusion
  (58 shorter events, 7.1 us)
Async XLA Ops:
  7.2 93.7 %copy-start = (bf16[640,2560]{1,0:T(8,128)(2,1)S(1)}, bf16[640,2560]{1,0:T(8,128)(2,1)}, u32[]{:S(2)}) copy-start(bf16[640,2560]{1,0:T(8,128)(2,1)} %param.18) | copy-start | bytes 9830404
  7.2 63.8 %copy-start.7 = (f32[2560]{0:T(1024)S(1)}, f32[2560]{0:T(1024)}, u32[]{:S(2)}) copy-start(f32[2560]{0:T(1024)} %param.16) | copy-start | bytes 30724
  7.2 63.7 %all-gather.5.cloned.1.call-start = ((), (), s32[]{:S(2)}) async-start(), calls=%async_computation.4 | async-start | bytes 5406720 | tf_op jit(solution)/shard_map/all_gather | solution.py:72
  21.0 116.7 %reduce-scatter.3.cloned.1.call-start = ((), (), s32[]{:S(2)}) async-start(), calls=%async_computation.5 | async-start | bytes 3276800 | tf_op jit(solution)/shard_map/reduce_scatter | solution.py:100
  85.2 1.9 slice-start.1
  85.2 2.9 slice-start
  88.8 7.8 %copy-start.5 = (bf16[512,160]{0,1:T(8,128)(2,1)S(1)}, bf16[512,160]{0,1:T(8,128)(2,1)}, u32[]{:S(2)}) copy-start(bf16[512,160]{0,1:T(8,128)(2,1)} %get-tuple-element.9) | copy-start | bytes 491524
  100.8 38.5 %copy-start.8 = (f32[2560]{0:T(1024)S(1)}, f32[2560]{0:T(1024)}, u32[]{:S(2)}) copy-start(f32[2560]{0:T(1024)} %param.17) | copy-start | bytes 30724
  104.6 78.2 %all-gather.7.cloned.1.call-start = ((), (), s32[]{:S(2)}) async-start(), calls=%async_computation.6 | async-start | bytes 3276800 | tf_op jit(solution)/shard_map/all_gather | solution.py:107
  139.3 8.1 %copy-start.2 = (f32[20,13824]{1,0:T(8,128)S(1)}, f32[20,13824]{1,0:T(8,128)}, u32[]{:S(2)}) copy-start(f32[20,13824]{1,0:T(8,128)} %param.15) | copy-start | bytes 3317764
  147.3 13.9 %copy-start.3 = (bf16[20,4,8,128]{3,2,1,0:T(8,128)(2,1)S(1)}, bf16[20,4,8,128]{3,2,1,0:T(8,128)(2,1)}, u32[]{:S(2)}) copy-start(bf16[20,4,8,128]{3,2,1,0:T(8,128)(2,1)} %get-tuple-element.8) | copy-start | bytes 491524
  147.3 14.0 %copy-start.4 = (bf16[512,2,40]{0,2,1:T(8,128)(2,1)S(1)}, bf16[512,2,40]{0,2,1:T(8,128)(2,1)}, u32[]{:S(2)}) copy-start(bf16[512,2,40]{0,2,1:T(8,128)(2,1)} %get-tuple-element.13) | copy-start | bytes 245764
  147.3 112.5 %all-gather.9.cloned.1.call-start = ((), (), s32[]{:S(2)}) async-start(), calls=%async_computation.7 | async-start | bytes 18247680 | tf_op jit(solution)/shard_map/all_gather | solution.py:73
  161.2 158.6 %all-gather.11.cloned.1.call-start = ((), (), s32[]{:S(2)}) async-start(), calls=%async_computation.9 | async-start | bytes 10813440 | tf_op jit(solution)/shard_map/all_gather | solution.py:135
  162.2 193.0 %reduce-scatter.5.cloned.1.call-start = ((), (), s32[]{:S(2)}) async-start(), calls=%async_computation.8 | async-start | bytes 3276800 | tf_op jit(solution)/shard_map/reduce_scatter | solution.py:111
  274.3 45.5 %copy-start.6 = (s32[128]{0:T(128)S(1)}, s32[128]{0:T(128)}, u32[]{:S(2)}) copy-start(s32[128]{0:T(128)} %param.12) | copy-start | bytes 1540
  319.8 38.0 %copy-start.1 = (bf16[640,2560]{1,0:T(8,128)(2,1)S(1)}, bf16[640,2560]{1,0:T(8,128)(2,1)}, u32[]{:S(2)}) copy-start(bf16[640,2560]{1,0:T(8,128)(2,1)} %param.18) | copy-start | bytes 9830404
Sparse Core Ops, SparseCore 0:
  21.2 49.7 all-gather.4
  104.7 32.9 reduce-scatter.2
  147.4 35.3 all-gather.6
  185.0 74.6 all-gather.8
  262.5 57.3 all-gather.10
  322.1 33.0 reduce-scatter.4

commit v2 on v1

v2 whole, which is shorter than its diff:
```python
import jax
import jax.numpy as jnp
from jax import lax
from jax.experimental import pallas as pl
from jax.experimental.pallas import tpu as pltpu
from jax.sharding import PartitionSpec as P

HD = 80
HALF = 40
PAGE = 128
MAIN = 16
BF = jnp.bfloat16
F32 = jnp.float32

eps_norm = 1e-05
theta_base = 10000.0

GATHER = 36
K_Q = 0
K_G = K_Q + GATHER
K_KV = K_G + GATHER
K_YQ = K_KV + GATHER
K_YG = K_YQ + 6
K_RS1 = K_YG + 6
K_AG = K_RS1 + 6
K_RS2 = K_AG + 6
N_SEM = K_RS2 + 6
STEPS = (0, -1, 1, 2)


def layer_kernel(
    length_ref,
    tok_hbm,
    tgt_ref,
    attn_gain_ref,
    ffn_gain_ref,
    qsrc_ref,
    gsrc_ref,
    outp_hbm,
    down_hbm,
    cos_ref,
    sin_ref,
    out_ref,
    pages_ref,
    wq,
    wg,
    place,
    outp,
    xh,
    xp,
    town,
    jt,
    qt,
    kk,
    vt,
    kv_own,
    ctxt,
    proj,
    hidden,
    keep,
    resid,
    rso,
    rsb,
    tq,
    tg,
    ssem,
    rsem,
    lsem,
):
    req = lax.axis_index("req")
    tp = lax.axis_index("tp")
    core = lax.rem(req, 2)
    x0 = lax.rem(lax.div(req, 2), 4)
    z0 = lax.div(req, 8)
    seq = xh.shape[0]
    dim = xh.shape[1]
    hcols = dim // 2
    rows80 = wq.shape[0] // 32
    length = length_ref[0]

    def member(a, b, c):
        z = lax.rem(z0 + 4 + c * a + (1 - c) * b, 4)
        x = lax.rem(x0 + 4 + (1 - c) * a + c * b, 4)
        return (z * 4 + x) * 2 + c

    def peer(a, b):
        return (member(a, b, core), tp)

    other = (member(0, 0, core) + 1 - 2 * core, tp)
    yp = lax.rem(tp + 1, 4)
    ym = lax.rem(tp + 3, 4)
    yo = lax.rem(tp + 2, 4)

    started = []

    def rc(src, dst, k, dev):
        return pltpu.make_async_remote_copy(
            src_ref=src,
            dst_ref=dst,
            send_sem=ssem.at[k],
            recv_sem=rsem.at[k],
            device_id=dev,
            device_id_type=pl.DeviceIdType.MESH,
        )

    def send(src, dst, k, dev):
        copy = rc(src, dst, k, dev)
        copy.start()
        started.append((k, copy))

    def arrive(dst, k):
        rc(dst, dst, k, other).wait_recv()

    loads = [
        pltpu.make_async_copy(tok_hbm, xh, lsem.at[0]),
        pltpu.make_async_copy(
            tok_hbm.at[pl.ds(pl.multiple_of(tp * 128, 128), 128), :], town, lsem.at[1]
        ),
        pltpu.make_async_copy(outp_hbm, outp, lsem.at[2]),
    ]
    for load in loads:
        load.start()

    barrier = pltpu.get_barrier_semaphore()
    friends = [peer(1, 0), peer(-1, 0), peer(0, 1), peer(0, -1), other]
    friends += [(req, yp), (req, ym), (req, yo)]
    for dev in friends:
        pl.semaphore_signal(
            barrier, inc=1, device_id=dev, device_id_type=pl.DeviceIdType.MESH
        )
    pl.semaphore_wait(barrier, len(friends))

    own80 = pl.multiple_of(req * rows80, 16)

    def main_rows(w, t):
        return w.at[pl.ds(pl.multiple_of(own80 + t * MAIN, MAIN), MAIN), :]

    gcols = wg.shape[1]

    def qpart(t, lo):
        return qsrc_ref.at[t, pl.ds(lo, MAIN), :]

    def gpart(t, lo):
        return gsrc_ref.at[pl.ds(lo, MAIN), pl.ds(pl.multiple_of(t * gcols, 128), gcols)]

    for part, w, tails, base in ((qpart, wq, tq, K_YQ), (gpart, wg, tg, K_YG)):
        for i, t in enumerate((yp, ym, yo)):
            send(part(t, 0), main_rows(w, tp), base + 2 * i, (req, t))
            send(part(t, MAIN), tails.at[tp], base + 2 * i + 1, (req, t))
    mine = []
    for part, w, tails, n in ((qpart, wq, tq, 3), (gpart, wg, tg, 5)):
        mine.append(pltpu.make_async_copy(part(tp, 0), main_rows(w, tp), lsem.at[n]))
        mine.append(pltpu.make_async_copy(part(tp, MAIN), tails.at[tp], lsem.at[n + 1]))
    for copy in mine:
        copy.start()

    def cross(w, tails, base, own):
        for copy in own:
            copy.wait()
        for i, t in enumerate((ym, yp, yo)):
            arrive(main_rows(w, t), base + 2 * i)
            arrive(tails.at[t], base + 2 * i + 1)
        tail = tails[0].astype(F32) + tails[1].astype(F32)
        tail = tail + (tails[2].astype(F32) + tails[3].astype(F32))
        w[pl.ds(pl.multiple_of(own80 + 4 * MAIN, MAIN), MAIN), :] = tail.astype(BF)

    class Gather:
        def __init__(self, first, block, base):
            self.first = first
            self.block = block
            self.base = base

        def at(self, a, b, part=None):
            return self.block(member(a, b, core), part)

        def push(self, i, j):
            a, b = STEPS[i], STEPS[j]
            src = self.first if (i, j, self.first is None) == (0, 0, False) else self.at(a, b)
            send(src, self.at(a, b), self.base + 20 + 4 * j + i, other)

        def src(self, a):
            return self.first if a == 0 and self.first is not None else self.at(a, 0)

        def second(self, i):
            a = STEPS[i]
            send(self.src(a), self.at(a, 0), self.base + 4 + i, peer(0, 1))
            send(self.src(a), self.at(a, 0), self.base + 8 + i, peer(0, -1))
            self.push(i, 0)

        def e0(self):
            send(self.src(0), self.at(0, 0), self.base, peer(1, 0))
            send(self.src(0), self.at(0, 0), self.base + 1, peer(-1, 0))
            self.second(0)

        def e1(self):
            arrive(self.at(-1, 0), self.base)
            send(self.at(-1, 0, 0), self.at(-1, 0, 0), self.base + 2, peer(1, 0))
            arrive(self.at(1, 0), self.base + 1)
            send(self.at(1, 0, 1), self.at(1, 0, 1), self.base + 3, peer(-1, 0))
            self.second(1)
            self.second(2)

        def e2(self):
            arrive(self.at(2, 0, 0), self.base + 2)
            arrive(self.at(2, 0, 1), self.base + 3)
            self.second(3)

        def e3(self, i):
            a = STEPS[i]
            arrive(self.at(a, -1), self.base + 4 + i)
            send(self.at(a, -1, 0), self.at(a, -1, 0), self.base + 12 + i, peer(0, 1))
            arrive(self.at(a, 1), self.base + 8 + i)
            send(self.at(a, 1, 1), self.at(a, 1, 1), self.base + 16 + i, peer(0, -1))
            self.push(i, 1)
            self.push(i, 2)

        def e4(self, i):
            a = STEPS[i]
            arrive(self.at(a, 2, 0), self.base + 12 + i)
            arrive(self.at(a, 2, 1), self.base + 16 + i)
            self.push(i, 3)

        def e5(self):
            for j in range(4):
                for i in range(4):
                    there = self.block(member(STEPS[i], STEPS[j], 1 - core), None)
                    arrive(there, self.base + 20 + 4 * j + i)

    def weight_block(w, cut):
        def block(owner, part):
            rows = pl.ds(pl.multiple_of(owner * rows80, 16), rows80)
            if part is None:
                return w.at[rows, :]
            if part == 0:
                return w.at[rows, pl.ds(0, cut)]
            return w.at[rows, pl.ds(cut, w.shape[1] - cut)]

        return block

    def page_block(owner, part):
        if part is None:
            return pages_ref.at[owner]
        return pages_ref.at[owner, pl.ds(part * (seq // 2), seq // 2), :]

    gat_q = Gather(None, weight_block(wq, 512), K_Q)
    gat_g = Gather(None, weight_block(wg, 1792), K_G)
    gat_kv = Gather(kv_own, page_block, K_KV)

    loads[0].wait()

    def norm_rows(i, carry):
        rows = pl.ds(pl.multiple_of(i * 64, 64), 64)
        v = xh[rows, :].astype(F32)
        scale = lax.rsqrt(jnp.mean(v * v, axis=-1, keepdims=True) + eps_norm)
        xh[rows, :] = (v * scale * attn_gain_ref[...]).astype(BF)
        return carry

    lax.fori_loop(0, seq // 64, norm_rows, 0)

    cross(wq, tq, K_YQ, mine[:2])
    gat_q.e0()

    def place_tile(i, carry):
        cols = pl.ds(pl.multiple_of(i * 256, 256), 256)

        def gen(r, c):
            here = r * 256 + lax.broadcasted_iota(jnp.int32, (256, 256), 0)
            hit = here == tgt_ref[:, cols]
            place[pl.ds(pl.multiple_of(r * 256, 256), 256), cols] = jnp.where(
                hit, 1.0, 0.0
            ).astype(BF)
            return c

        lax.fori_loop(0, dim // 256, gen, 0)
        xp[:, cols] = jnp.dot(
            xh[...], place[:, cols], preferred_element_type=F32
        ).astype(BF)
        return carry

    lax.fori_loop(0, 2, place_tile, 0)
    gat_q.e1()
    lax.fori_loop(2, 4, place_tile, 0)
    gat_q.e2()
    gat_q.e3(0)
    lax.fori_loop(4, 6, place_tile, 0)
    gat_q.e3(1)
    gat_q.e3(2)
    lax.fori_loop(6, 8, place_tile, 0)
    gat_q.e3(3)
    gat_q.e4(0)
    lax.fori_loop(8, 10, place_tile, 0)
    cross(wg, tg, K_YG, mine[2:])
    gat_g.e0()
    gat_q.e4(1)
    gat_q.e4(2)
    gat_q.e4(3)
    gat_q.e5()

    def joined_tile(i, carry):
        cols = pl.ds(pl.multiple_of(i * 256, 256), 256)
        tile = jnp.dot(xp[...], wq[:, cols], preferred_element_type=F32)
        jt[pl.ds(pl.multiple_of(i * 256, 256), 256), :] = tile.T
        return carry

    lax.fori_loop(0, 3, joined_tile, 0)
    jt[768:960, :] = jnp.dot(xp[...], wq[:, 768:960], preferred_element_type=F32).T

    heads, groups = 8, 2
    cosine, sine = cos_ref[...], sin_ref[...]
    for h in range(heads + groups):
        first = jt[h * HD : h * HD + HALF, :]
        second = jt[h * HD + HALF : (h + 1) * HD, :]
        turned = jnp.concatenate(
            [first * cosine - second * sine, second * cosine + first * sine], axis=0
        )
        if h < heads:
            qt[h * HD : (h + 1) * HD, :] = turned.astype(BF)
        else:
            jt[h * HD : (h + 1) * HD, :] = turned
            kk[h - heads] = turned.T.astype(BF)
    vt[...] = jt[800:960, :].astype(BF)
    kv_rows = jt[640:960, :].T
    live_rows = lax.broadcasted_iota(jnp.int32, kv_rows.shape, 0) < length
    kv_own[...] = jnp.where(live_rows, kv_rows, 0.0).astype(BF)
    gat_g.e1()

    def attend(blk):
        at = pl.multiple_of(blk * 128, 128)
        for g in range(groups):
            q4 = jnp.concatenate(
                [
                    qt[(4 * g + h) * HD : (4 * g + h + 1) * HD, pl.ds(at, 128)]
                    for h in range(4)
                ],
                axis=1,
            )
            s = jnp.dot(kk[g], q4, preferred_element_type=F32) * HD ** (-0.5)
            key = lax.broadcasted_iota(jnp.int32, s.shape, 0)
            slot = lax.rem(lax.broadcasted_iota(jnp.int32, s.shape, 1), 128) + at
            s = jnp.where((key <= slot) & (key < length), s, -1e30)
            e = jnp.exp(s - jnp.max(s, axis=0, keepdims=True))
            probs = (e * (1.0 / jnp.sum(e, axis=0, keepdims=True))).astype(BF)
            c = jnp.dot(
                vt[g * HD : (g + 1) * HD, :], probs, preferred_element_type=F32
            )
            for h in range(4):
                ctxt[(4 * g + h) * HD : (4 * g + h + 1) * HD, :] = c[
                    :, h * 128 : (h + 1) * 128
                ]
        return ctxt[...].T.astype(BF)

    def rows_of(blk):
        return pl.ds(pl.multiple_of(blk * 128, 128), 128)

    lo, hi = pl.ds(0, hcols), pl.ds(hcols, hcols)

    def far_half(left, blk, base, half):
        xp[rows_of(yo), half] = blk.astype(BF)
        if left:
            send(xp.at[rows_of(yo), half], rso.at[0], base, (req, ym))
        else:
            send(xp.at[rows_of(yo), half], rso.at[1], base + 1, (req, yp))

    def near_up(a_part, b_part, base):
        xp[rows_of(yp), lo] = a_part.astype(BF)
        send(xp.at[rows_of(yp), lo], rsb.at[0, :, lo], base + 2, (req, yp))
        keep[0] = b_part

    def near_down(a_part, b_part, base):
        xp[rows_of(ym), hi] = b_part.astype(BF)
        send(xp.at[rows_of(ym), hi], rsb.at[1, :, hi], base + 3, (req, ym))
        keep[1] = a_part

    def near_combine(base):
        arrive(rso.at[1], base + 1)
        xp[rows_of(yp), hi] = (keep[0] + rso[1].astype(F32)).astype(BF)
        send(xp.at[rows_of(yp), hi], rsb.at[0, :, hi], base + 4, (req, yp))
        arrive(rso.at[0], base)
        xp[rows_of(ym), lo] = (keep[1] + rso[0].astype(F32)).astype(BF)
        send(xp.at[rows_of(ym), lo], rsb.at[1, :, lo], base + 5, (req, ym))

    def near_done(base):
        arrive(rsb.at[0, :, lo], base + 2)
        arrive(rsb.at[1, :, hi], base + 3)
        arrive(rsb.at[0, :, hi], base + 4)
        arrive(rsb.at[1, :, lo], base + 5)

    def out_half(ctx, half):
        return jnp.dot(ctx, outp[:, half], preferred_element_type=F32)

    loads[2].wait()
    ctx = attend(yo)
    far_half(True, out_half(ctx, lo), K_RS1, lo)
    far_half(False, out_half(ctx, hi), K_RS1, hi)
    gat_g.e2()
    ctx = attend(yp)
    near_up(out_half(ctx, lo), out_half(ctx, hi), K_RS1)
    gat_g.e3(0)
    ctx = attend(ym)
    near_down(out_half(ctx, lo), out_half(ctx, hi), K_RS1)
    near_combine(K_RS1)
    gat_g.e3(1)
    loads[1].wait()
    ctx = attend(tp)
    resid[:, lo] = out_half(ctx, lo) + town[:, lo].astype(F32)
    resid[:, hi] = out_half(ctx, hi) + town[:, hi].astype(F32)
    gat_g.e3(2)
    near_done(K_RS1)

    total = resid[...] + rsb[0].astype(F32) + rsb[1].astype(F32)
    resid[...] = total
    scale = lax.rsqrt(jnp.mean(total * total, axis=-1, keepdims=True) + eps_norm)
    h_own = (total * scale * ffn_gain_ref[...]).astype(BF)
    hidden[0:128, 0:hcols] = h_own[:, 0:hcols]
    hidden[128:256, 0:hcols] = h_own[:, hcols:dim]

    def order_tile(i, carry):
        cols = pl.ds(pl.multiple_of(i * 256, 256), 256)
        tile = jnp.dot(
            hidden[0:128, 0:hcols], place[0:hcols, cols], preferred_element_type=F32
        )
        tile = tile + jnp.dot(
            hidden[128:256, 0:hcols], place[hcols:dim, cols], preferred_element_type=F32
        )
        xh[rows_of(tp), cols] = tile.astype(BF)
        return carry

    lax.fori_loop(0, 5, order_tile, 0)
    send(xh.at[rows_of(tp), lo], xh.at[rows_of(tp), lo], K_AG, (req, yp))
    lax.fori_loop(5, 10, order_tile, 0)
    send(xh.at[rows_of(tp), hi], xh.at[rows_of(tp), hi], K_AG + 1, (req, ym))
    send(xh.at[rows_of(tp), hi], xh.at[rows_of(tp), hi], K_AG + 2, (req, yp))
    send(xh.at[rows_of(tp), lo], xh.at[rows_of(tp), lo], K_AG + 3, (req, ym))

    down = place.at[0 : down_hbm.shape[0], :]
    load_down = pltpu.make_async_copy(down_hbm, down, lsem.at[7])
    load_down.start()
    gat_g.e3(3)
    gat_g.e4(0)
    gat_g.e4(1)
    gat_g.e4(2)
    gat_g.e4(3)
    gat_kv.e0()
    own_pages = pltpu.make_async_copy(kv_own, pages_ref.at[req], lsem.at[8])
    own_pages.start()
    arrive(xh.at[rows_of(ym), lo], K_AG)
    send(xh.at[rows_of(ym), lo], xh.at[rows_of(ym), lo], K_AG + 4, (req, yp))
    arrive(xh.at[rows_of(yp), hi], K_AG + 1)
    send(xh.at[rows_of(yp), hi], xh.at[rows_of(yp), hi], K_AG + 5, (req, ym))
    gat_g.e5()
    load_down.wait()

    ff = down_hbm.shape[0]

    def gate_up(blk):
        rows = rows_of(blk)

        def tile(i, carry):
            cols = pl.ds(pl.multiple_of(i * 256, 256), 256)
            proj[:, cols] = jnp.dot(xh[rows, :], wg[:, cols], preferred_element_type=F32)
            return carry

        lax.fori_loop(0, 13, tile, 0)
        proj[:, 3328:3456] = jnp.dot(
            xh[rows, :], wg[:, 3328:3456], preferred_element_type=F32
        )
        gate = proj[:, 0:ff]
        up = proj[:, ff : 2 * ff]
        hidden[rows, :] = (gate * jax.nn.sigmoid(gate) * up).astype(BF)

    def down_half(blk, half):
        return jnp.dot(
            hidden[rows_of(blk), :], down[:, half], preferred_element_type=F32
        )

    gate_up(tp)
    resid[:, lo] = resid[:, lo] + down_half(tp, lo)
    resid[:, hi] = resid[:, hi] + down_half(tp, hi)
    gat_kv.e1()
    for k, copy in started:
        if K_RS1 <= k < K_RS1 + 6:
            copy.wait_send()
    arrive(xh.at[rows_of(yp), lo], K_AG + 3)
    gate_up(yp)
    near_up(down_half(yp, lo), down_half(yp, hi), K_RS2)
    gat_kv.e2()
    gat_kv.e3(0)
    arrive(xh.at[rows_of(ym), hi], K_AG + 2)
    gate_up(ym)
    near_down(down_half(ym, lo), down_half(ym, hi), K_RS2)
    gat_kv.e3(1)
    arrive(xh.at[rows_of(yo), lo], K_AG + 4)
    arrive(xh.at[rows_of(yo), hi], K_AG + 5)
    gate_up(yo)
    far_half(True, down_half(yo, lo), K_RS2, lo)
    far_half(False, down_half(yo, hi), K_RS2, hi)
    gat_kv.e3(2)
    gat_kv.e3(3)
    near_combine(K_RS2)
    gat_kv.e4(0)
    gat_kv.e4(1)
    gat_kv.e4(2)
    gat_kv.e4(3)
    near_done(K_RS2)
    live = (lax.broadcasted_iota(jnp.int32, (128, 1), 0) + tp * 128) < length
    total = resid[...] + rsb[0].astype(F32) + rsb[1].astype(F32)
    out_ref[...] = jnp.where(live, total, 0.0).astype(BF)
    gat_kv.e5()
    own_pages.wait()
    for k, copy in started:
        if not K_RS1 <= k < K_RS1 + 6:
            copy.wait_send()


def pick_kernel(idx_ref, page_ref, out_ref):
    out_ref[...] = page_ref[...]


def packed(shard, tp):
    tail = jnp.tile(shard[MAIN:], (4, 1))
    here = jnp.arange(MAIN, dtype=jnp.int32)[:, None] // 4 == tp
    return jnp.concatenate([shard[:MAIN], jnp.where(here, tail, 0.0)], axis=0).astype(BF)


def body(
    tokens,
    lengths,
    page_slot,
    trainer_layout,
    trainer_qkv,
    trainer_gateup,
    attn_gain,
    ffn_gain,
    out_proj,
    down_proj,
):
    req = lax.axis_index("req")
    tp = lax.axis_index("tp")
    seq, dim = tokens.shape
    gcols = trainer_gateup.shape[1] // 4
    qcols = trainer_qkv.shape[1] // 4
    rows_each = trainer_qkv.shape[0]
    ff = down_proj.shape[0]
    kvc = 320
    qsrc = packed(trainer_qkv, tp).reshape(2 * MAIN, 4, qcols).transpose(1, 0, 2)
    gsrc = packed(trainer_gateup, tp)
    first_row = (trainer_layout * rows_each).reshape(32, 4, 1)
    tgt = jnp.concatenate(
        [
            (first_row + jnp.arange(MAIN, dtype=jnp.int32)).reshape(32, 4 * MAIN),
            (first_row + jnp.arange(MAIN, rows_each, dtype=jnp.int32)).reshape(32, -1),
        ],
        axis=1,
    ).reshape(1, dim)
    freq = theta_base ** (-jnp.arange(HALF, dtype=F32) * 2.0 / HD)
    angles = freq[:, None] * jnp.arange(seq, dtype=F32)[None, :]
    vmem = pl.BlockSpec(memory_space=pltpu.VMEM)
    anywhere = pl.BlockSpec(memory_space=pl.ANY)
    layer_out, pages = pl.pallas_call(
        layer_kernel,
        out_shape=(
            jax.ShapeDtypeStruct((seq // 4, dim), BF),
            jax.ShapeDtypeStruct((32, seq, kvc), BF),
        ),
        in_specs=[
            pl.BlockSpec(memory_space=pltpu.SMEM),
            anywhere,
            vmem,
            vmem,
            vmem,
            vmem,
            vmem,
            anywhere,
            anywhere,
            vmem,
            vmem,
        ],
        out_specs=(vmem, anywhere),
        scratch_shapes=[
            pltpu.VMEM((dim, qcols), BF),
            pltpu.VMEM((dim, gcols), BF),
            pltpu.VMEM((dim, dim), BF),
            pltpu.VMEM(out_proj.shape, BF),
            pltpu.VMEM((seq, dim), BF),
            pltpu.VMEM((seq, dim), BF),
            pltpu.VMEM((seq // 4, dim), BF),
            pltpu.VMEM((qcols, seq), F32),
            pltpu.VMEM((8 * HD, seq), BF),
            pltpu.VMEM((2, seq, HD), BF),
            pltpu.VMEM((2 * HD, seq), BF),
            pltpu.VMEM((seq, kvc), BF),
            pltpu.VMEM((8 * HD, 128), F32),
            pltpu.VMEM((128, gcols), F32),
            pltpu.VMEM((seq, ff), BF),
            pltpu.VMEM((2, 128, dim // 2), F32),
            pltpu.VMEM((128, dim), F32),
            pltpu.VMEM((2, 128, dim // 2), BF),
            pltpu.VMEM((2, 128, dim), BF),
            pltpu.VMEM((4, MAIN, qcols), BF),
            pltpu.VMEM((4, MAIN, gcols), BF),
            pltpu.SemaphoreType.DMA((N_SEM,)),
            pltpu.SemaphoreType.DMA((N_SEM,)),
            pltpu.SemaphoreType.DMA((9,)),
        ],
        compiler_params=pltpu.CompilerParams(
            collective_id=0, has_side_effects=True, vmem_limit_bytes=67043328
        ),
        name="layer",
    )(
        lengths,
        tokens,
        tgt,
        attn_gain.reshape(1, dim),
        ffn_gain.reshape(1, dim),
        qsrc,
        gsrc,
        out_proj,
        down_proj,
        jnp.cos(angles),
        jnp.sin(angles),
    )
    per = seq // PAGE
    slots = req * per + jnp.arange(per, dtype=jnp.int32)
    number = jnp.arange(page_slot.shape[0], dtype=jnp.int32)
    idx = jnp.sum(
        jnp.where(page_slot[None, :] == slots[:, None], number[None, :], 0), axis=1
    ).astype(jnp.int32)
    kv_cache = pl.pallas_call(
        pick_kernel,
        out_shape=jax.ShapeDtypeStruct((per, PAGE, kvc), BF),
        grid_spec=pltpu.PrefetchScalarGridSpec(
            num_scalar_prefetch=1,
            grid=(per,),
            in_specs=[pl.BlockSpec((1, PAGE, kvc), lambda i, ids: (ids[i], 0, 0))],
            out_specs=pl.BlockSpec((1, PAGE, kvc), lambda i, ids: (i, 0, 0)),
        ),
        name="pick",
    )(idx, pages.reshape(32 * per, PAGE, kvc))
    return (layer_out, kv_cache)


def solution(mesh):
    return jax.shard_map(
        body,
        mesh=mesh,
        in_specs=(
            P("req", None),
            P("req"),
            P(),
            P(),
            P(("req", "tp"), None),
            P(("req", "tp"), None),
            P(),
            P(),
            P("tp", None),
            P("tp", None),
        ),
        out_specs=(P(("req", "tp"), None), P("req", None, "tp")),
        check_vma=False,
    )
```

time: 365 us -> 155 us (0.42)
  waiting for transfers between devices: 236 us -> 0 us
  Pallas kernels: 0 us -> 134 us
  matrix products: 72.3 us -> 0 us
  blocking collectives: 22.4 us -> 0 us
  between operations: 15 us -> 1.4 us
  other arithmetic: 14.1 us -> 5.36 us
  local copies, waits for them, and re-layouts: 4.84 us -> 11.4 us
    all_gather x4 -> x0, waiting for transfers between devices: 178 us -> none  [the longest x1 76.9 us: body(): gu_weight = lax.all_gather(gu_half, 'req', axis=0, tiled=True)]
    pallas_call x0 -> x2, Pallas kernels: none -> 134 us  [the longest x1 130 us: body(): pl.pallas_call(layer_kernel, out_shape=(jax.ShapeDtypeStruct((seq // 4, d...]
    dot_general x7 -> x0, matrix products: 64.5 us -> none  [the longest x1 14.5 us: body(): projected = jnp.dot(h_norm, gu_weight, preferred_element_type=jnp.float32)]
    reduce_scatter x2 -> x0, waiting for transfers between devices: 57.9 us -> none  [the longest x1 33 us: body(): lax.psum_scatter(partial_out.astype(jnp.bfloat16), 'tp', scatter_dimensio...]
    all_to_all x2 -> x0, blocking collectives: 22.4 us -> none  [the longest x1 12.4 us: body(): lax.all_to_all(trainer_gateup.astype(jnp.bfloat16), 'tp', split_axis=1, c...]
    sub x1 -> x0, matrix products: 7.77 us -> none  [body(): probs = jax.nn.softmax(scores, axis=-1).astype(jnp.bfloat16)]
    slice x4, local copies, waits for them, and re-layouts: 0.01 us -> 4.13 us  [the longest x2 2.18 us: packed(): shard[:MAIN]]
    convert_element_type x5 -> x0, other arithmetic: 3.84 us -> none  [the longest x1 2.6 us: body(): ((resid_share + added) * live_share[:, None]).astype(jnp.bfloat16)]
  transfers between devices with their start and end apart: 6 -> 0, of which waited for: 6 -> 0; matrix products, arithmetic and copies ran while one was open for 11% -> 0% of each run, Pallas kernels for 0% -> 0%
where the time goes in v2:
time: 155 us; the launch traced here: 152 us
  Pallas kernels  134 us (86%)
  local copies, waits for them, and re-layouts  11.4 us (7%)
  other arithmetic  5.36 us (3%)
    pallas_call x1, Pallas kernels, body(): pl.pallas_call(layer_kernel, out_shape=(jax.ShapeDtypeStruct((seq // 4, d...  130 us
    pallas_call x1, Pallas kernels, body(): pl.pallas_call(pick_kernel, out_shape=jax.ShapeDtypeStruct((per, PAGE, kv...  3.91 us

profile of v2, /device:TPU:1, one launch (start us, length us, event | category | flops | bytes accessed | tf_op | source)
XLA Modules:
  0.0 152.1 jit_solution(9197056916541390565)
XLA Ops:
  1.3 1.4 select_reduce_fusion.idx_ref
  2.7 0.7 broadcast_multiply_fusion
  3.6 1.3 reshape.96.attn_gain_ref
  4.9 1.3 reshape.97.ffn_gain_ref
  6.2 0.1 add.65
  6.7 0.1 pad_add_fusion
  6.8 0.7 reshape.95.tgt_ref
  7.5 0.9 slice.15
  8.4 0.2 tile.9
  8.6 0.1 fusion
  8.7 1.0 slice.17
  9.8 1.0 slice.23
  10.7 0.2 concatenate.15
  11.0 0.7 maximum_bitcast_fusion.qsrc_ref
  11.7 1.0 fusion.1
  12.7 0.1 tile.20
  12.9 0.1 tile.21
  13.0 0.1 select_convert_fusion
  13.1 1.2 slice.22
  14.3 1.0 pad_maximum_fusion.gsrc_ref
  15.4 130.1 %layer.1 = (bf16[128,2560]{1,0:T(8,128)(2,1)}, bf16[32,512,320]{2,1,0:T(8,128)(2,1)}) custom-call(s32[1]{0:T(128)S(6)} %copy.37.length_ref, bf16[512,2560]{1,0:T(8,128)(2,1)} %tok_hbm.1, s32[1,2560]{1,0:T(1,128)} %reshape.95.tgt_ref, f32[1,2560]{1,0:T(1,128)} %reshape.96.attn_gain_ref, f32[1,2560]{1,0:T(1,128)} %reshape.97.ffn_gain_ref, ...), custom_call_target="tpu_custom_call" | custom-call | tf_op jit(solution)/shard_map/layer/pallas_call | solution.py:559
  145.5 3.9 %pick.1 = bf16[4,128,320]{2,1,0:T(8,128)(2,1)} custom-call(s32[4]{0:T(128)} %select_reduce_fusion.idx_ref, bf16[128,128,320]{2,1,0:T(8,128)(2,1)} %bitcast.6), custom_call_target="tpu_custom_call" | custom-call | tf_op jit(solution)/shard_map/pick/pallas_call | solution.py:628
  149.4 1.9 %copy.32 = bf16[4,128,320]{1,2,0:T(8,128)(2,1)} copy(bf16[4,128,320]{2,1,0:T(8,128)(2,1)} %pick.1) | data formatting | bytes 655360
  151.3 0.8 copy.38
  (18 shorter events, 0.7 us)
Async XLA Ops:
  145.5 5.8 %copy-start = (bf16[128,2560]{1,0:T(8,128)(2,1)S(1)}, bf16[128,2560]{1,0:T(8,128)(2,1)}, u32[]{:S(2)}) copy-start(bf16[128,2560]{1,0:T(8,128)(2,1)} %get-tuple-element.18) | copy-start | bytes 1966084

commit v3 on v2

--- a/solution.py
+++ b/solution.py
@@ -1,5 +1,6 @@
 import jax
 import jax.numpy as jnp
+import numpy as np
 from jax import lax
 from jax.experimental import pallas as pl
 from jax.experimental.pallas import tpu as pltpu
@@ -22,26 +23,33 @@
 K_YQ = K_KV + GATHER
 K_YG = K_YQ + 6
 K_RS1 = K_YG + 6
-K_AG = K_RS1 + 6
+K_AG = K_RS1 + 10
 K_RS2 = K_AG + 6
-N_SEM = K_RS2 + 6
+N_SEM = K_RS2 + 10
 STEPS = (0, -1, 1, 2)
 
 
 def layer_kernel(
     length_ref,
+    slot_ref,
     tok_hbm,
-    tgt_ref,
+    layout_ref,
     attn_gain_ref,
     ffn_gain_ref,
-    qsrc_ref,
-    gsrc_ref,
+    q_hbm,
+    g_hbm,
     outp_hbm,
     down_hbm,
     cos_ref,
     sin_ref,
     out_ref,
     pages_ref,
+    idx_ref,
+    qf,
+    gf,
+    qsrc_ref,
+    gsrc_ref,
+    tgt_ref,
     wq,
     wg,
     place,
@@ -55,7 +63,6 @@
     vt,
     kv_own,
     ctxt,
-    proj,
     hidden,
     keep,
     resid,
@@ -111,6 +118,21 @@
     def arrive(dst, k):
         rc(dst, dst, k, other).wait_recv()
 
+    barrier = pltpu.get_barrier_semaphore()
+    friends = [peer(1, 0), peer(-1, 0), peer(0, 1), peer(0, -1), other]
+    friends += [(req, yp), (req, ym), (req, yo)]
+    for dev in friends:
+        pl.semaphore_signal(
+            barrier, inc=1, device_id=dev, device_id_type=pl.DeviceIdType.MESH
+        )
+
+    gcols = wg.shape[1]
+    shard = [
+        pltpu.make_async_copy(q_hbm, qf, lsem.at[9]),
+        pltpu.make_async_copy(g_hbm, gf, lsem.at[10]),
+    ]
+    for load in shard:
+        load.start()
     loads = [
         pltpu.make_async_copy(tok_hbm, xh, lsem.at[0]),
         pltpu.make_async_copy(
@@ -121,13 +143,24 @@
     for load in loads:
         load.start()
 
-    barrier = pltpu.get_barrier_semaphore()
-    friends = [peer(1, 0), peer(-1, 0), peer(0, 1), peer(0, -1), other]
-    friends += [(req, yp), (req, ym), (req, yo)]
-    for dev in friends:
-        pl.semaphore_signal(
-            barrier, inc=1, device_id=dev, device_id_type=pl.DeviceIdType.MESH
-        )
+    def pack(wide, tall, put):
+        put(0, wide.astype(BF))
+        row = lax.broadcasted_iota(jnp.int32, (MAIN, wide.shape[1]), 0)
+        tail = jnp.zeros(row.shape, F32)
+        for i in range(4):
+            tail = jnp.where(row == 4 * tp + i, tall[i : i + 1, :], tail)
+        put(MAIN, tail.astype(BF))
+
+    qcols = wq.shape[1]
+    shard[0].wait()
+    for t in range(4):
+        span = slice(t * qcols, (t + 1) * qcols)
+
+        def put_q(lo, v, t=t):
+            qsrc_ref[t, lo : lo + MAIN, :] = v
+
+        pack(qf[0:MAIN, span], qf[MAIN:20, span], put_q)
+
     pl.semaphore_wait(barrier, len(friends))
 
     own80 = pl.multiple_of(req * rows80, 16)
@@ -135,24 +168,58 @@
     def main_rows(w, t):
         return w.at[pl.ds(pl.multiple_of(own80 + t * MAIN, MAIN), MAIN), :]
 
-    gcols = wg.shape[1]
-
     def qpart(t, lo):
         return qsrc_ref.at[t, pl.ds(lo, MAIN), :]
 
     def gpart(t, lo):
         return gsrc_ref.at[pl.ds(lo, MAIN), pl.ds(pl.multiple_of(t * gcols, 128), gcols)]
 
-    for part, w, tails, base in ((qpart, wq, tq, K_YQ), (gpart, wg, tg, K_YG)):
+    mine = []
+
+    def spread(part, w, tails, base, n):
         for i, t in enumerate((yp, ym, yo)):
             send(part(t, 0), main_rows(w, tp), base + 2 * i, (req, t))
             send(part(t, MAIN), tails.at[tp], base + 2 * i + 1, (req, t))
-    mine = []
-    for part, w, tails, n in ((qpart, wq, tq, 3), (gpart, wg, tg, 5)):
         mine.append(pltpu.make_async_copy(part(tp, 0), main_rows(w, tp), lsem.at[n]))
         mine.append(pltpu.make_async_copy(part(tp, MAIN), tails.at[tp], lsem.at[n + 1]))
-    for copy in mine:
-        copy.start()
+        mine[-2].start()
+        mine[-1].start()
+
+    spread(qpart, wq, tq, K_YQ, 3)
+
+    def paired(w):
+        gate, up = w[:, : gcols // 2], w[:, gcols // 2 :]
+        tiles = []
+        for i in range(0, gcols // 2, 128):
+            tiles += [gate[:, i : i + 128], up[:, i : i + 128]]
+        return jnp.concatenate(tiles, axis=1)
+
+    shard[1].wait()
+    for t in range(4):
+        span = slice(t * gcols, (t + 1) * gcols)
+
+        def put_g(lo, v, span=span):
+            gsrc_ref[lo : lo + MAIN, span] = v
+
+        pack(paired(gf[0:MAIN, span]), paired(gf[MAIN:20, span]), put_g)
+    spread(gpart, wg, tg, K_YG, 5)
+
+    col = lax.broadcasted_iota(jnp.int32, (1, dim), 1)
+    owner = lax.shift_right_logical(lax.shift_right_logical(col, 4) * 205, 10)
+    inside = col - owner * rows80
+    in_main = inside < 4 * MAIN
+    over = inside - 4 * MAIN
+    from_tp = jnp.where(
+        in_main, lax.shift_right_logical(inside, 4), lax.shift_right_logical(over, 2)
+    )
+    row_in = jnp.where(in_main, inside & 15, MAIN + (over & 3))
+    pick = lax.broadcasted_iota(jnp.int32, (128, dim), 0) == owner * 4 + from_tp
+    block = jnp.dot(
+        jnp.broadcast_to(layout_ref[...], (8, 128)).astype(F32).astype(BF),
+        jnp.where(pick, 1.0, 0.0).astype(BF),
+        preferred_element_type=F32,
+    )
+    tgt_ref[...] = block[0:1, :].astype(jnp.int32) * 20 + row_in
 
     def cross(w, tails, base, own):
         for copy in own:
@@ -240,7 +307,7 @@
     def page_block(owner, part):
         if part is None:
             return pages_ref.at[owner]
-        return pages_ref.at[owner, pl.ds(part * (seq // 2), seq // 2), :]
+        return pages_ref.at[owner, pl.ds(part * 2, 2)]
 
     gat_q = Gather(None, weight_block(wq, 512), K_Q)
     gat_g = Gather(None, weight_block(wg, 1792), K_G)
@@ -252,13 +319,10 @@
         rows = pl.ds(pl.multiple_of(i * 64, 64), 64)
         v = xh[rows, :].astype(F32)
         scale = lax.rsqrt(jnp.mean(v * v, axis=-1, keepdims=True) + eps_norm)
-        xh[rows, :] = (v * scale * attn_gain_ref[...]).astype(BF)
+        xh[rows, :] = (v * scale * attn_gain_ref[...][None, :]).astype(BF)
         return carry
 
     lax.fori_loop(0, seq // 64, norm_rows, 0)
-
-    cross(wq, tq, K_YQ, mine[:2])
-    gat_q.e0()
 
     def place_tile(i, carry):
         cols = pl.ds(pl.multiple_of(i * 256, 256), 256)
@@ -277,20 +341,24 @@
         ).astype(BF)
         return carry
 
-    lax.fori_loop(0, 2, place_tile, 0)
+    lax.fori_loop(0, 1, place_tile, 0)
+    cross(wq, tq, K_YQ, mine[:2])
+    gat_q.e0()
+    lax.fori_loop(1, 4, place_tile, 0)
     gat_q.e1()
-    lax.fori_loop(2, 4, place_tile, 0)
-    gat_q.e2()
     gat_q.e3(0)
     lax.fori_loop(4, 6, place_tile, 0)
+    gat_q.e2()
+    lax.fori_loop(6, 7, place_tile, 0)
     gat_q.e3(1)
     gat_q.e3(2)
-    lax.fori_loop(6, 8, place_tile, 0)
+    lax.fori_loop(7, 8, place_tile, 0)
+    gat_q.e4(0)
+    lax.fori_loop(8, 9, place_tile, 0)
     gat_q.e3(3)
-    gat_q.e4(0)
-    lax.fori_loop(8, 10, place_tile, 0)
     cross(wg, tg, K_YG, mine[2:])
     gat_g.e0()
+    lax.fori_loop(9, 10, place_tile, 0)
     gat_q.e4(1)
     gat_q.e4(2)
     gat_q.e4(3)
@@ -319,9 +387,19 @@
             jt[h * HD : (h + 1) * HD, :] = turned
             kk[h - heads] = turned.T.astype(BF)
     vt[...] = jt[800:960, :].astype(BF)
-    kv_rows = jt[640:960, :].T
-    live_rows = lax.broadcasted_iota(jnp.int32, kv_rows.shape, 0) < length
-    kv_own[...] = jnp.where(live_rows, kv_rows, 0.0).astype(BF)
+    for j in range(4):
+        slot = lax.broadcasted_iota(jnp.int32, (320, 128), 1) + j * 128
+        kv_own[j] = jnp.where(
+            slot < length, jt[640:960, j * 128 : (j + 1) * 128], 0.0
+        ).astype(BF)
+
+    def find(n, found):
+        here = slot_ref[n] - req * 4
+        return tuple(jnp.where(here == d, n, f) for d, f in enumerate(found))
+
+    found = lax.fori_loop(0, 128, find, (0, 0, 0, 0))
+    for d in range(4):
+        idx_ref[d] = found[d]
     gat_g.e1()
 
     def attend(blk):
@@ -354,36 +432,46 @@
 
     lo, hi = pl.ds(0, hcols), pl.ds(hcols, hcols)
 
+    def slot(i, c=None):
+        if c is None:
+            return pl.ds(128 * i, 128)
+        return pl.ds(128 * i + 64 * c, 64)
+
     def far_half(left, blk, base, half):
-        xp[rows_of(yo), half] = blk.astype(BF)
-        if left:
-            send(xp.at[rows_of(yo), half], rso.at[0], base, (req, ym))
-        else:
-            send(xp.at[rows_of(yo), half], rso.at[1], base + 1, (req, yp))
+        xp[slot(3), half] = blk.astype(BF)
+        for c in range(2):
+            k = base + c + (0 if left else 2)
+            dst = rso.at[0 if left else 1, slot(0, c), :]
+            send(xp.at[slot(3, c), half], dst, k, (req, ym if left else yp))
 
     def near_up(a_part, b_part, base):
-        xp[rows_of(yp), lo] = a_part.astype(BF)
-        send(xp.at[rows_of(yp), lo], rsb.at[0, :, lo], base + 2, (req, yp))
+        xp[slot(1), lo] = a_part.astype(BF)
+        send(xp.at[slot(1), lo], rsb.at[0, :, lo], base + 4, (req, yp))
         keep[0] = b_part
 
     def near_down(a_part, b_part, base):
-        xp[rows_of(ym), hi] = b_part.astype(BF)
-        send(xp.at[rows_of(ym), hi], rsb.at[1, :, hi], base + 3, (req, ym))
+        xp[slot(2), hi] = b_part.astype(BF)
+        send(xp.at[slot(2), hi], rsb.at[1, :, hi], base + 5, (req, ym))
         keep[1] = a_part
 
     def near_combine(base):
-        arrive(rso.at[1], base + 1)
-        xp[rows_of(yp), hi] = (keep[0] + rso[1].astype(F32)).astype(BF)
-        send(xp.at[rows_of(yp), hi], rsb.at[0, :, hi], base + 4, (req, yp))
-        arrive(rso.at[0], base)
-        xp[rows_of(ym), lo] = (keep[1] + rso[0].astype(F32)).astype(BF)
-        send(xp.at[rows_of(ym), lo], rsb.at[1, :, lo], base + 5, (req, ym))
+        for c in range(2):
+            part = slot(0, c)
+            arrive(rso.at[1, part, :], base + 2 + c)
+            both = keep[0, part, :] + rso[1, part, :].astype(F32)
+            xp[slot(1, c), hi] = both.astype(BF)
+            send(xp.at[slot(1, c), hi], rsb.at[0, part, hi], base + 6 + c, (req, yp))
+            arrive(rso.at[0, part, :], base + c)
+            both = keep[1, part, :] + rso[0, part, :].astype(F32)
+            xp[slot(2, c), lo] = both.astype(BF)
+            send(xp.at[slot(2, c), lo], rsb.at[1, part, lo], base + 8 + c, (req, ym))
 
     def near_done(base):
-        arrive(rsb.at[0, :, lo], base + 2)
-        arrive(rsb.at[1, :, hi], base + 3)
-        arrive(rsb.at[0, :, hi], base + 4)
-        arrive(rsb.at[1, :, lo], base + 5)
+        arrive(rsb.at[0, :, lo], base + 4)
+        arrive(rsb.at[1, :, hi], base + 5)
+        for c in range(2):
+            arrive(rsb.at[0, slot(0, c), hi], base + 6 + c)
+            arrive(rsb.at[1, slot(0, c), lo], base + 8 + c)
 
     def out_half(ctx, half):
         return jnp.dot(ctx, outp[:, half], preferred_element_type=F32)
@@ -392,10 +480,10 @@
     ctx = attend(yo)
     far_half(True, out_half(ctx, lo), K_RS1, lo)
     far_half(False, out_half(ctx, hi), K_RS1, hi)
-    gat_g.e2()
+    gat_g.e3(0)
     ctx = attend(yp)
     near_up(out_half(ctx, lo), out_half(ctx, hi), K_RS1)
-    gat_g.e3(0)
+    gat_g.e2()
     ctx = attend(ym)
     near_down(out_half(ctx, lo), out_half(ctx, hi), K_RS1)
     near_combine(K_RS1)
@@ -405,12 +493,14 @@
     resid[:, lo] = out_half(ctx, lo) + town[:, lo].astype(F32)
     resid[:, hi] = out_half(ctx, hi) + town[:, hi].astype(F32)
     gat_g.e3(2)
+    gat_g.e4(0)
+    gat_g.e3(3)
     near_done(K_RS1)
 
     total = resid[...] + rsb[0].astype(F32) + rsb[1].astype(F32)
     resid[...] = total
     scale = lax.rsqrt(jnp.mean(total * total, axis=-1, keepdims=True) + eps_norm)
-    h_own = (total * scale * ffn_gain_ref[...]).astype(BF)
+    h_own = (total * scale * ffn_gain_ref[...][None, :]).astype(BF)
     hidden[0:128, 0:hcols] = h_own[:, 0:hcols]
     hidden[128:256, 0:hcols] = h_own[:, hcols:dim]
 
@@ -422,81 +512,91 @@
         tile = tile + jnp.dot(
             hidden[128:256, 0:hcols], place[hcols:dim, cols], preferred_element_type=F32
         )
-        xh[rows_of(tp), cols] = tile.astype(BF)
+        xh[0:128, cols] = tile.astype(BF)
         return carry
 
     lax.fori_loop(0, 5, order_tile, 0)
-    send(xh.at[rows_of(tp), lo], xh.at[rows_of(tp), lo], K_AG, (req, yp))
+    send(xh.at[slot(0), lo], xh.at[slot(2), lo], K_AG, (req, yp))
+    send(xh.at[slot(0), lo], xh.at[slot(1), lo], K_AG + 1, (req, ym))
     lax.fori_loop(5, 10, order_tile, 0)
-    send(xh.at[rows_of(tp), hi], xh.at[rows_of(tp), hi], K_AG + 1, (req, ym))
-    send(xh.at[rows_of(tp), hi], xh.at[rows_of(tp), hi], K_AG + 2, (req, yp))
-    send(xh.at[rows_of(tp), lo], xh.at[rows_of(tp), lo], K_AG + 3, (req, ym))
+    send(xh.at[slot(0), hi], xh.at[slot(2), hi], K_AG + 2, (req, yp))
+    send(xh.at[slot(0), hi], xh.at[slot(1), hi], K_AG + 3, (req, ym))
 
     down = place.at[0 : down_hbm.shape[0], :]
     load_down = pltpu.make_async_copy(down_hbm, down, lsem.at[7])
     load_down.start()
-    gat_g.e3(3)
-    gat_g.e4(0)
     gat_g.e4(1)
     gat_g.e4(2)
     gat_g.e4(3)
     gat_kv.e0()
     own_pages = pltpu.make_async_copy(kv_own, pages_ref.at[req], lsem.at[8])
     own_pages.start()
-    arrive(xh.at[rows_of(ym), lo], K_AG)
-    send(xh.at[rows_of(ym), lo], xh.at[rows_of(ym), lo], K_AG + 4, (req, yp))
-    arrive(xh.at[rows_of(yp), hi], K_AG + 1)
-    send(xh.at[rows_of(yp), hi], xh.at[rows_of(yp), hi], K_AG + 5, (req, ym))
+    arrive(xh.at[slot(2), lo], K_AG)
+    send(xh.at[slot(2), lo], xh.at[slot(3), lo], K_AG + 4, (req, yp))
     gat_g.e5()
     load_down.wait()
 
     ff = down_hbm.shape[0]
 
-    def gate_up(blk):
-        rows = rows_of(blk)
+    def gate_up(first, count):
+        rows = pl.ds(128 * first, 128 * count)
 
         def tile(i, carry):
-            cols = pl.ds(pl.multiple_of(i * 256, 256), 256)
-            proj[:, cols] = jnp.dot(xh[rows, :], wg[:, cols], preferred_element_type=F32)
+            both = jnp.dot(
+                xh[rows, :],
+                wg[:, pl.ds(pl.multiple_of(i * 256, 256), 256)],
+                preferred_element_type=F32,
+            )
+            gate, up = both[:, :128], both[:, 128:]
+            hidden[rows, pl.ds(pl.multiple_of(i * 128, 128), 128)] = (
+                gate * jax.nn.sigmoid(gate) * up
+            ).astype(BF)
             return carry
 
         lax.fori_loop(0, 13, tile, 0)
-        proj[:, 3328:3456] = jnp.dot(
-            xh[rows, :], wg[:, 3328:3456], preferred_element_type=F32
+        both = jnp.dot(xh[rows, :], wg[:, 3328:3456], preferred_element_type=F32)
+        up = pltpu.roll(both, 64, 1)
+        last = (both * jax.nn.sigmoid(both) * up).astype(BF)
+        hidden[rows, 1664:1728] = last[:, :64]
+
+    def down_half(first, count, half):
+        return jnp.dot(
+            hidden[pl.ds(128 * first, 128 * count), :],
+            down[:, half],
+            preferred_element_type=F32,
         )
-        gate = proj[:, 0:ff]
-        up = proj[:, ff : 2 * ff]
-        hidden[rows, :] = (gate * jax.nn.sigmoid(gate) * up).astype(BF)
-
-    def down_half(blk, half):
-        return jnp.dot(
-            hidden[rows_of(blk), :], down[:, half], preferred_element_type=F32
-        )
-
-    gate_up(tp)
-    resid[:, lo] = resid[:, lo] + down_half(tp, lo)
-    resid[:, hi] = resid[:, hi] + down_half(tp, hi)
+
+    gate_up(0, 1)
+    resid[:, lo] = resid[:, lo] + down_half(0, 1, lo)
+    resid[:, hi] = resid[:, hi] + down_half(0, 1, hi)
+    arrive(xh.at[slot(1), hi], K_AG + 3)
+    send(xh.at[slot(1), hi], xh.at[slot(3), hi], K_AG + 5, (req, ym))
     gat_kv.e1()
     for k, copy in started:
-        if K_RS1 <= k < K_RS1 + 6:
+        if K_RS1 <= k < K_RS1 + 10:
             copy.wait_send()
-    arrive(xh.at[rows_of(yp), lo], K_AG + 3)
-    gate_up(yp)
-    near_up(down_half(yp, lo), down_half(yp, hi), K_RS2)
+    arrive(xh.at[slot(1), lo], K_AG + 1)
+    arrive(xh.at[slot(2), hi], K_AG + 2)
+    gate_up(1, 2)
+    part = down_half(1, 2, lo)
+    xp[slot(1), lo] = part[0:128].astype(BF)
+    send(xp.at[slot(1), lo], rsb.at[0, :, lo], K_RS2 + 4, (req, yp))
+    keep[1] = part[128:256]
+    part = down_half(1, 2, hi)
+    xp[slot(2), hi] = part[128:256].astype(BF)
+    send(xp.at[slot(2), hi], rsb.at[1, :, hi], K_RS2 + 5, (req, ym))
+    keep[0] = part[0:128]
     gat_kv.e2()
     gat_kv.e3(0)
-    arrive(xh.at[rows_of(ym), hi], K_AG + 2)
-    gate_up(ym)
-    near_down(down_half(ym, lo), down_half(ym, hi), K_RS2)
+    arrive(xh.at[slot(3), lo], K_AG + 4)
+    arrive(xh.at[slot(3), hi], K_AG + 5)
+    gate_up(3, 1)
+    far_half(True, down_half(3, 1, lo), K_RS2, lo)
+    far_half(False, down_half(3, 1, hi), K_RS2, hi)
     gat_kv.e3(1)
-    arrive(xh.at[rows_of(yo), lo], K_AG + 4)
-    arrive(xh.at[rows_of(yo), hi], K_AG + 5)
-    gate_up(yo)
-    far_half(True, down_half(yo, lo), K_RS2, lo)
-    far_half(False, down_half(yo, hi), K_RS2, hi)
     gat_kv.e3(2)
+    near_combine(K_RS2)
     gat_kv.e3(3)
-    near_combine(K_RS2)
     gat_kv.e4(0)
     gat_kv.e4(1)
     gat_kv.e4(2)
@@ -508,18 +608,19 @@
     gat_kv.e5()
     own_pages.wait()
     for k, copy in started:
-        if not K_RS1 <= k < K_RS1 + 6:
+        if not K_RS1 <= k < K_RS1 + 10:
             copy.wait_send()
 
 
-def pick_kernel(idx_ref, page_ref, out_ref):
-    out_ref[...] = page_ref[...]
-
-
-def packed(shard, tp):
-    tail = jnp.tile(shard[MAIN:], (4, 1))
-    here = jnp.arange(MAIN, dtype=jnp.int32)[:, None] // 4 == tp
-    return jnp.concatenate([shard[:MAIN], jnp.where(here, tail, 0.0)], axis=0).astype(BF)
+def pick_kernel(idx_ref, pages_ref, out_ref, sem):
+    copies = [
+        pltpu.make_async_copy(pages_ref.at[idx_ref[d]], out_ref.at[d], sem.at[d])
+        for d in range(4)
+    ]
+    for copy in copies:
+        copy.start()
+    for copy in copies:
+        copy.wait()
 
 
 def body(
@@ -534,49 +635,44 @@
     out_proj,
     down_proj,
 ):
-    req = lax.axis_index("req")
-    tp = lax.axis_index("tp")
     seq, dim = tokens.shape
     gcols = trainer_gateup.shape[1] // 4
     qcols = trainer_qkv.shape[1] // 4
-    rows_each = trainer_qkv.shape[0]
     ff = down_proj.shape[0]
-    kvc = 320
-    qsrc = packed(trainer_qkv, tp).reshape(2 * MAIN, 4, qcols).transpose(1, 0, 2)
-    gsrc = packed(trainer_gateup, tp)
-    first_row = (trainer_layout * rows_each).reshape(32, 4, 1)
-    tgt = jnp.concatenate(
-        [
-            (first_row + jnp.arange(MAIN, dtype=jnp.int32)).reshape(32, 4 * MAIN),
-            (first_row + jnp.arange(MAIN, rows_each, dtype=jnp.int32)).reshape(32, -1),
-        ],
-        axis=1,
-    ).reshape(1, dim)
-    freq = theta_base ** (-jnp.arange(HALF, dtype=F32) * 2.0 / HD)
-    angles = freq[:, None] * jnp.arange(seq, dtype=F32)[None, :]
+    per = seq // PAGE
+    freq = theta_base ** (-np.arange(HALF, dtype=np.float32) * 2.0 / HD)
+    angles = freq.astype(np.float32)[:, None] * np.arange(seq, dtype=np.float32)[None, :]
     vmem = pl.BlockSpec(memory_space=pltpu.VMEM)
     anywhere = pl.BlockSpec(memory_space=pl.ANY)
-    layer_out, pages = pl.pallas_call(
+    smem = pl.BlockSpec(memory_space=pltpu.SMEM)
+    layer_out, pages, idx = pl.pallas_call(
         layer_kernel,
         out_shape=(
             jax.ShapeDtypeStruct((seq // 4, dim), BF),
-            jax.ShapeDtypeStruct((32, seq, kvc), BF),
+            jax.ShapeDtypeStruct((32, per, 320, PAGE), BF),
+            jax.ShapeDtypeStruct((4,), jnp.int32),
         ),
         in_specs=[
-            pl.BlockSpec(memory_space=pltpu.SMEM),
+            smem,
+            smem,
             anywhere,
-            vmem,
-            vmem,
             vmem,
             vmem,
             vmem,
             anywhere,
             anywhere,
+            anywhere,
+            anywhere,
             vmem,
             vmem,
         ],
-        out_specs=(vmem, anywhere),
+        out_specs=(vmem, anywhere, smem),
         scratch_shapes=[
+            pltpu.VMEM(trainer_qkv.shape, F32),
+            pltpu.VMEM(trainer_gateup.shape, F32),
+            pltpu.VMEM((4, 2 * MAIN, qcols), BF),
+            pltpu.VMEM((2 * MAIN, 4 * gcols), BF),
+            pltpu.VMEM((1, dim), jnp.int32),
             pltpu.VMEM((dim, qcols), BF),
             pltpu.VMEM((dim, gcols), BF),
             pltpu.VMEM((dim, dim), BF),
@@ -588,9 +684,8 @@
             pltpu.VMEM((8 * HD, seq), BF),
             pltpu.VMEM((2, seq, HD), BF),
             pltpu.VMEM((2 * HD, seq), BF),
-            pltpu.VMEM((seq, kvc), BF),
+            pltpu.VMEM((per, 320, PAGE), BF),
             pltpu.VMEM((8 * HD, 128), F32),
-            pltpu.VMEM((128, gcols), F32),
             pltpu.VMEM((seq, ff), BF),
             pltpu.VMEM((2, 128, dim // 2), F32),
             pltpu.VMEM((128, dim), F32),
@@ -600,7 +695,7 @@
             pltpu.VMEM((4, MAIN, gcols), BF),
             pltpu.SemaphoreType.DMA((N_SEM,)),
             pltpu.SemaphoreType.DMA((N_SEM,)),
-            pltpu.SemaphoreType.DMA((9,)),
+            pltpu.SemaphoreType.DMA((11,)),
         ],
         compiler_params=pltpu.CompilerParams(
             collective_id=0, has_side_effects=True, vmem_limit_bytes=67043328
@@ -608,34 +703,27 @@
         name="layer",
     )(
         lengths,
+        page_slot,
         tokens,
-        tgt,
-        attn_gain.reshape(1, dim),
-        ffn_gain.reshape(1, dim),
-        qsrc,
-        gsrc,
+        trainer_layout.reshape(1, -1),
+        attn_gain,
+        ffn_gain,
+        trainer_qkv,
+        trainer_gateup,
         out_proj,
         down_proj,
-        jnp.cos(angles),
-        jnp.sin(angles),
+        jnp.asarray(np.cos(angles), F32),
+        jnp.asarray(np.sin(angles), F32),
     )
-    per = seq // PAGE
-    slots = req * per + jnp.arange(per, dtype=jnp.int32)
-    number = jnp.arange(page_slot.shape[0], dtype=jnp.int32)
-    idx = jnp.sum(
-        jnp.where(page_slot[None, :] == slots[:, None], number[None, :], 0), axis=1
-    ).astype(jnp.int32)
-    kv_cache = pl.pallas_call(
+    pool = pl.pallas_call(
         pick_kernel,
-        out_shape=jax.ShapeDtypeStruct((per, PAGE, kvc), BF),
-        grid_spec=pltpu.PrefetchScalarGridSpec(
-            num_scalar_prefetch=1,
-            grid=(per,),
-            in_specs=[pl.BlockSpec((1, PAGE, kvc), lambda i, ids: (ids[i], 0, 0))],
-            out_specs=pl.BlockSpec((1, PAGE, kvc), lambda i, ids: (i, 0, 0)),
-        ),
+        out_shape=jax.ShapeDtypeStruct((per, 320, PAGE), BF),
+        in_specs=[smem, anywhere],
+        out_specs=vmem,
+        scratch_shapes=[pltpu.SemaphoreType.DMA((4,))],
         name="pick",
-    )(idx, pages.reshape(32 * per, PAGE, kvc))
+    )(idx, pages.reshape(32 * per, 320, PAGE))
+    kv_cache = pool.transpose(0, 2, 1)
     return (layer_out, kv_cache)
 
 

time: 155 us -> 133 us (0.86); the launches traced: 152 us -> 133 us
  local copies, waits for them, and re-layouts: 11.4 us -> 0.84 us
  other arithmetic: 5.36 us -> 0 us
  Pallas kernels: 134 us -> 131 us
    slice x4 -> x0, local copies, waits for them, and re-layouts: 4.13 us -> none  [the longest x2 2.18 us: packed(): shard[:MAIN]]
    reshape x3 -> x0, local copies, waits for them, and re-layouts: 3.31 us -> none  [the longest x1 1.31 us: body(): attn_gain.reshape(1, dim)]
    pallas_call x1, Pallas kernels: 130 us -> 128 us  [body(): pl.pallas_call(layer_kernel, out_shape=(jax.ShapeDtypeStruct((seq // 4, d...]
    unnamed x4 -> x3, local copies, waits for them, and re-layouts: 2.73 us -> 0.84 us
where the time goes in v3:
time: 133 us
  Pallas kernels  131 us (98%)
    pallas_call x1, Pallas kernels, body(): pl.pallas_call(layer_kernel, out_shape=(jax.ShapeDtypeStruct((seq // 4, d...  128 us

profile of v3, /device:TPU:1, one launch (start us, length us, event | category | flops | bytes accessed | tf_op | source)
XLA Modules:
  0.0 132.8 jit_solution(16082469488427985903)
XLA Ops:
  1.3 128.0 %layer.1 = (bf16[128,2560]{1,0:T(8,128)(2,1)}, bf16[32,4,320,128]{3,2,1,0:T(8,128)(2,1)}, s32[4]{0:T(128)}) custom-call(s32[1]{0:T(128)S(6)} %copy.15.length_ref, s32[128]{0:T(128)} %slot_ref.1, bf16[512,2560]{1,0:T(8,128)(2,1)} %tok_hbm.1, s32[1,128]{1,0:T(1,128)} %bitcast.5, f32[2560]{0:T(1024)} %attn_gain_ref.1, f32[2560]{0:T(1024)} %ffn_gain_ref.1, ...), custom_call_target="tpu_custom_call" | custom-call | tf_op jit(solution)/shard_map/layer/pallas_call | solution.py:648
  129.3 0.0 copy-start
  129.3 2.6 %pick.1 = bf16[4,320,128]{2,1,0:T(8,128)(2,1)} custom-call(s32[4]{0:T(128)} %get-tuple-element.6.idx_ref, bf16[128,320,128]{2,1,0:T(8,128)(2,1)} %bitcast.3), custom_call_target="tpu_custom_call" | custom-call | tf_op jit(solution)/shard_map/pick/pallas_call | solution.py:718
  131.9 0.0 copy-done
  131.9 0.8 copy.16
Async XLA Ops:
  129.3 2.6 %copy-start = (bf16[128,2560]{1,0:T(8,128)(2,1)S(1)}, bf16[128,2560]{1,0:T(8,128)(2,1)}, u32[]{:S(2)}) copy-start(bf16[128,2560]{1,0:T(8,128)(2,1)} %get-tuple-element.10) | copy-start | bytes 1966084

commit v4 on v3

--- a/solution.py
+++ b/solution.py
@@ -56,9 +56,9 @@
     outp,
     xh,
     xp,
+    stage,
     town,
     jt,
-    qt,
     kk,
     vt,
     kv_own,
@@ -187,22 +187,16 @@
 
     spread(qpart, wq, tq, K_YQ, 3)
 
-    def paired(w):
-        gate, up = w[:, : gcols // 2], w[:, gcols // 2 :]
-        tiles = []
-        for i in range(0, gcols // 2, 128):
-            tiles += [gate[:, i : i + 128], up[:, i : i + 128]]
-        return jnp.concatenate(tiles, axis=1)
-
-    shard[1].wait()
-    for t in range(4):
-        span = slice(t * gcols, (t + 1) * gcols)
-
-        def put_g(lo, v, span=span):
-            gsrc_ref[lo : lo + MAIN, span] = v
-
-        pack(paired(gf[0:MAIN, span]), paired(gf[MAIN:20, span]), put_g)
-    spread(gpart, wg, tg, K_YG, 5)
+    loads[0].wait()
+
+    def norm_rows(i, carry):
+        rows = pl.ds(pl.multiple_of(i * 64, 64), 64)
+        v = xh[rows, :].astype(F32)
+        scale = lax.rsqrt(jnp.mean(v * v, axis=-1, keepdims=True) + eps_norm)
+        xh[rows, :] = (v * scale * attn_gain_ref[...][None, :]).astype(BF)
+        return carry
+
+    lax.fori_loop(0, seq // 64, norm_rows, 0)
 
     col = lax.broadcasted_iota(jnp.int32, (1, dim), 1)
     owner = lax.shift_right_logical(lax.shift_right_logical(col, 4) * 205, 10)
@@ -264,6 +258,7 @@
             send(self.at(-1, 0, 0), self.at(-1, 0, 0), self.base + 2, peer(1, 0))
             arrive(self.at(1, 0), self.base + 1)
             send(self.at(1, 0, 1), self.at(1, 0, 1), self.base + 3, peer(-1, 0))
+            self.e3(0)
             self.second(1)
             self.second(2)
 
@@ -313,17 +308,6 @@
     gat_g = Gather(None, weight_block(wg, 1792), K_G)
     gat_kv = Gather(kv_own, page_block, K_KV)
 
-    loads[0].wait()
-
-    def norm_rows(i, carry):
-        rows = pl.ds(pl.multiple_of(i * 64, 64), 64)
-        v = xh[rows, :].astype(F32)
-        scale = lax.rsqrt(jnp.mean(v * v, axis=-1, keepdims=True) + eps_norm)
-        xh[rows, :] = (v * scale * attn_gain_ref[...][None, :]).astype(BF)
-        return carry
-
-    lax.fori_loop(0, seq // 64, norm_rows, 0)
-
     def place_tile(i, carry):
         cols = pl.ds(pl.multiple_of(i * 256, 256), 256)
 
@@ -341,57 +325,66 @@
         ).astype(BF)
         return carry
 
-    lax.fori_loop(0, 1, place_tile, 0)
     cross(wq, tq, K_YQ, mine[:2])
     gat_q.e0()
-    lax.fori_loop(1, 4, place_tile, 0)
+    def paired(w):
+        gate, up = w[:, : gcols // 2], w[:, gcols // 2 :]
+        tiles = []
+        for i in range(0, gcols // 2, 128):
+            tiles += [gate[:, i : i + 128], up[:, i : i + 128]]
+        return jnp.concatenate(tiles, axis=1)
+
+    shard[1].wait()
+    for t in range(4):
+        span = slice(t * gcols, (t + 1) * gcols)
+
+        def put_g(lo, v, span=span):
+            gsrc_ref[lo : lo + MAIN, span] = v
+
+        pack(paired(gf[0:MAIN, span]), paired(gf[MAIN:20, span]), put_g)
+    spread(gpart, wg, tg, K_YG, 5)
+
+    lax.fori_loop(0, 2, place_tile, 0)
     gat_q.e1()
-    gat_q.e3(0)
+    lax.fori_loop(2, 4, place_tile, 0)
+    gat_q.e2()
     lax.fori_loop(4, 6, place_tile, 0)
-    gat_q.e2()
-    lax.fori_loop(6, 7, place_tile, 0)
     gat_q.e3(1)
     gat_q.e3(2)
-    lax.fori_loop(7, 8, place_tile, 0)
+    lax.fori_loop(6, 8, place_tile, 0)
     gat_q.e4(0)
     lax.fori_loop(8, 9, place_tile, 0)
     gat_q.e3(3)
     cross(wg, tg, K_YG, mine[2:])
     gat_g.e0()
-    lax.fori_loop(9, 10, place_tile, 0)
     gat_q.e4(1)
     gat_q.e4(2)
+    lax.fori_loop(9, 10, place_tile, 0)
     gat_q.e4(3)
     gat_q.e5()
 
-    def joined_tile(i, carry):
-        cols = pl.ds(pl.multiple_of(i * 256, 256), 256)
-        tile = jnp.dot(xp[...], wq[:, cols], preferred_element_type=F32)
-        jt[pl.ds(pl.multiple_of(i * 256, 256), 256), :] = tile.T
-        return carry
-
-    lax.fori_loop(0, 3, joined_tile, 0)
-    jt[768:960, :] = jnp.dot(xp[...], wq[:, 768:960], preferred_element_type=F32).T
-
     heads, groups = 8, 2
-    cosine, sine = cos_ref[...], sin_ref[...]
-    for h in range(heads + groups):
-        first = jt[h * HD : h * HD + HALF, :]
-        second = jt[h * HD + HALF : (h + 1) * HD, :]
-        turned = jnp.concatenate(
+    qwide = heads * HD
+    jt[...] = jnp.dot(xp[...], wq[:, qwide:], preferred_element_type=F32).T
+
+    def turn(rows, cosine, sine):
+        first, second = rows[:HALF, :], rows[HALF:, :]
+        return jnp.concatenate(
             [first * cosine - second * sine, second * cosine + first * sine], axis=0
         )
-        if h < heads:
-            qt[h * HD : (h + 1) * HD, :] = turned.astype(BF)
-        else:
-            jt[h * HD : (h + 1) * HD, :] = turned
-            kk[h - heads] = turned.T.astype(BF)
-    vt[...] = jt[800:960, :].astype(BF)
-    for j in range(4):
-        slot = lax.broadcasted_iota(jnp.int32, (320, 128), 1) + j * 128
-        kv_own[j] = jnp.where(
-            slot < length, jt[640:960, j * 128 : (j + 1) * 128], 0.0
-        ).astype(BF)
+
+    for g in range(groups):
+        turned = turn(jt[g * HD : (g + 1) * HD, :], cos_ref[...], sin_ref[...])
+        jt[g * HD : (g + 1) * HD, :] = turned
+        kk[g] = turned.T.astype(BF)
+    vt[...] = jt[2 * HD : 4 * HD, :].astype(BF)
+
+    def keep_pages():
+        for j in range(4):
+            slots = lax.broadcasted_iota(jnp.int32, (320, 128), 1) + j * 128
+            kv_own[j] = jnp.where(
+                slots < length, jt[:, j * 128 : (j + 1) * 128], 0.0
+            ).astype(BF)
 
     def find(n, found):
         here = slot_ref[n] - req * 4
@@ -400,18 +393,19 @@
     found = lax.fori_loop(0, 128, find, (0, 0, 0, 0))
     for d in range(4):
         idx_ref[d] = found[d]
-    gat_g.e1()
 
     def attend(blk):
         at = pl.multiple_of(blk * 128, 128)
+        own = jnp.dot(
+            xp[pl.ds(at, 128), :], wq[:, 0:qwide], preferred_element_type=F32
+        ).T
+        cosine, sine = cos_ref[:, pl.ds(at, 128)], sin_ref[:, pl.ds(at, 128)]
+        query = [
+            turn(own[h * HD : (h + 1) * HD, :], cosine, sine).astype(BF)
+            for h in range(heads)
+        ]
         for g in range(groups):
-            q4 = jnp.concatenate(
-                [
-                    qt[(4 * g + h) * HD : (4 * g + h + 1) * HD, pl.ds(at, 128)]
-                    for h in range(4)
-                ],
-                axis=1,
-            )
+            q4 = jnp.concatenate(query[4 * g : 4 * g + 4], axis=1)
             s = jnp.dot(kk[g], q4, preferred_element_type=F32) * HD ** (-0.5)
             key = lax.broadcasted_iota(jnp.int32, s.shape, 0)
             slot = lax.rem(lax.broadcasted_iota(jnp.int32, s.shape, 1), 128) + at
@@ -438,20 +432,20 @@
         return pl.ds(128 * i + 64 * c, 64)
 
     def far_half(left, blk, base, half):
-        xp[slot(3), half] = blk.astype(BF)
+        stage[slot(2), half] = blk.astype(BF)
         for c in range(2):
             k = base + c + (0 if left else 2)
             dst = rso.at[0 if left else 1, slot(0, c), :]
-            send(xp.at[slot(3, c), half], dst, k, (req, ym if left else yp))
+            send(stage.at[slot(2, c), half], dst, k, (req, ym if left else yp))
 
     def near_up(a_part, b_part, base):
-        xp[slot(1), lo] = a_part.astype(BF)
-        send(xp.at[slot(1), lo], rsb.at[0, :, lo], base + 4, (req, yp))
+        stage[slot(0), lo] = a_part.astype(BF)
+        send(stage.at[slot(0), lo], rsb.at[0, :, lo], base + 4, (req, yp))
         keep[0] = b_part
 
     def near_down(a_part, b_part, base):
-        xp[slot(2), hi] = b_part.astype(BF)
-        send(xp.at[slot(2), hi], rsb.at[1, :, hi], base + 5, (req, ym))
+        stage[slot(1), hi] = b_part.astype(BF)
+        send(stage.at[slot(1), hi], rsb.at[1, :, hi], base + 5, (req, ym))
         keep[1] = a_part
 
     def near_combine(base):
@@ -459,12 +453,12 @@
             part = slot(0, c)
             arrive(rso.at[1, part, :], base + 2 + c)
             both = keep[0, part, :] + rso[1, part, :].astype(F32)
-            xp[slot(1, c), hi] = both.astype(BF)
-            send(xp.at[slot(1, c), hi], rsb.at[0, part, hi], base + 6 + c, (req, yp))
+            stage[slot(0, c), hi] = both.astype(BF)
+            send(stage.at[slot(0, c), hi], rsb.at[0, part, hi], base + 6 + c, (req, yp))
             arrive(rso.at[0, part, :], base + c)
             both = keep[1, part, :] + rso[0, part, :].astype(F32)
-            xp[slot(2, c), lo] = both.astype(BF)
-            send(xp.at[slot(2, c), lo], rsb.at[1, part, lo], base + 8 + c, (req, ym))
+            stage[slot(1, c), lo] = both.astype(BF)
+            send(stage.at[slot(1, c), lo], rsb.at[1, part, lo], base + 8 + c, (req, ym))
 
     def near_done(base):
         arrive(rsb.at[0, :, lo], base + 4)
@@ -480,21 +474,19 @@
     ctx = attend(yo)
     far_half(True, out_half(ctx, lo), K_RS1, lo)
     far_half(False, out_half(ctx, hi), K_RS1, hi)
-    gat_g.e3(0)
     ctx = attend(yp)
     near_up(out_half(ctx, lo), out_half(ctx, hi), K_RS1)
-    gat_g.e2()
     ctx = attend(ym)
     near_down(out_half(ctx, lo), out_half(ctx, hi), K_RS1)
-    near_combine(K_RS1)
-    gat_g.e3(1)
+    gat_g.e1()
     loads[1].wait()
     ctx = attend(tp)
     resid[:, lo] = out_half(ctx, lo) + town[:, lo].astype(F32)
     resid[:, hi] = out_half(ctx, hi) + town[:, hi].astype(F32)
-    gat_g.e3(2)
-    gat_g.e4(0)
-    gat_g.e3(3)
+    near_combine(K_RS1)
+    gat_g.e2()
+    keep_pages()
+    gat_g.e3(1)
     near_done(K_RS1)
 
     total = resid[...] + rsb[0].astype(F32) + rsb[1].astype(F32)
@@ -525,20 +517,19 @@
     down = place.at[0 : down_hbm.shape[0], :]
     load_down = pltpu.make_async_copy(down_hbm, down, lsem.at[7])
     load_down.start()
-    gat_g.e4(1)
-    gat_g.e4(2)
-    gat_g.e4(3)
-    gat_kv.e0()
     own_pages = pltpu.make_async_copy(kv_own, pages_ref.at[req], lsem.at[8])
     own_pages.start()
+    gat_g.e3(2)
+    gat_g.e3(3)
+    gat_kv.e0()
     arrive(xh.at[slot(2), lo], K_AG)
     send(xh.at[slot(2), lo], xh.at[slot(3), lo], K_AG + 4, (req, yp))
-    gat_g.e5()
-    load_down.wait()
+    for i in range(4):
+        gat_g.e4(i)
 
     ff = down_hbm.shape[0]
 
-    def gate_up(first, count):
+    def gate_up(first, count, between):
         rows = pl.ds(128 * first, 128 * count)
 
         def tile(i, carry):
@@ -553,7 +544,9 @@
             ).astype(BF)
             return carry
 
-        lax.fori_loop(0, 13, tile, 0)
+        lax.fori_loop(0, 7, tile, 0)
+        between()
+        lax.fori_loop(7, 13, tile, 0)
         both = jnp.dot(xh[rows, :], wg[:, 3328:3456], preferred_element_type=F32)
         up = pltpu.roll(both, 64, 1)
         last = (both * jax.nn.sigmoid(both) * up).astype(BF)
@@ -566,46 +559,43 @@
             preferred_element_type=F32,
         )
 
-    gate_up(0, 1)
-    resid[:, lo] = resid[:, lo] + down_half(0, 1, lo)
-    resid[:, hi] = resid[:, hi] + down_half(0, 1, hi)
     arrive(xh.at[slot(1), hi], K_AG + 3)
     send(xh.at[slot(1), hi], xh.at[slot(3), hi], K_AG + 5, (req, ym))
-    gat_kv.e1()
+    gat_g.e5()
+    load_down.wait()
     for k, copy in started:
         if K_RS1 <= k < K_RS1 + 10:
             copy.wait_send()
     arrive(xh.at[slot(1), lo], K_AG + 1)
     arrive(xh.at[slot(2), hi], K_AG + 2)
-    gate_up(1, 2)
+    gate_up(1, 2, gat_kv.e1)
     part = down_half(1, 2, lo)
-    xp[slot(1), lo] = part[0:128].astype(BF)
-    send(xp.at[slot(1), lo], rsb.at[0, :, lo], K_RS2 + 4, (req, yp))
+    stage[slot(0), lo] = part[0:128].astype(BF)
+    send(stage.at[slot(0), lo], rsb.at[0, :, lo], K_RS2 + 4, (req, yp))
     keep[1] = part[128:256]
     part = down_half(1, 2, hi)
-    xp[slot(2), hi] = part[128:256].astype(BF)
-    send(xp.at[slot(2), hi], rsb.at[1, :, hi], K_RS2 + 5, (req, ym))
+    stage[slot(1), hi] = part[128:256].astype(BF)
+    send(stage.at[slot(1), hi], rsb.at[1, :, hi], K_RS2 + 5, (req, ym))
     keep[0] = part[0:128]
     gat_kv.e2()
-    gat_kv.e3(0)
     arrive(xh.at[slot(3), lo], K_AG + 4)
     arrive(xh.at[slot(3), hi], K_AG + 5)
-    gate_up(3, 1)
+    gate_up(3, 1, lambda: gat_kv.e3(1))
     far_half(True, down_half(3, 1, lo), K_RS2, lo)
     far_half(False, down_half(3, 1, hi), K_RS2, hi)
-    gat_kv.e3(1)
     gat_kv.e3(2)
+    gat_kv.e4(0)
+    gate_up(0, 1, lambda: gat_kv.e3(3))
+    resid[:, lo] = resid[:, lo] + down_half(0, 1, lo)
+    resid[:, hi] = resid[:, hi] + down_half(0, 1, hi)
     near_combine(K_RS2)
-    gat_kv.e3(3)
-    gat_kv.e4(0)
-    gat_kv.e4(1)
-    gat_kv.e4(2)
-    gat_kv.e4(3)
+    for i in range(1, 4):
+        gat_kv.e4(i)
     near_done(K_RS2)
     live = (lax.broadcasted_iota(jnp.int32, (128, 1), 0) + tp * 128) < length
     total = resid[...] + rsb[0].astype(F32) + rsb[1].astype(F32)
+    gat_kv.e5()
     out_ref[...] = jnp.where(live, total, 0.0).astype(BF)
-    gat_kv.e5()
     own_pages.wait()
     for k, copy in started:
         if not K_RS1 <= k < K_RS1 + 10:
@@ -679,9 +669,9 @@
             pltpu.VMEM(out_proj.shape, BF),
             pltpu.VMEM((seq, dim), BF),
             pltpu.VMEM((seq, dim), BF),
+            pltpu.VMEM((384, dim), BF),
             pltpu.VMEM((seq // 4, dim), BF),
-            pltpu.VMEM((qcols, seq), F32),
-            pltpu.VMEM((8 * HD, seq), BF),
+            pltpu.VMEM((4 * HD, seq), F32),
             pltpu.VMEM((2, seq, HD), BF),
             pltpu.VMEM((2 * HD, seq), BF),
             pltpu.VMEM((per, 320, PAGE), BF),

time: 133 us -> 132 us (level)
  no operation moved by 1% of the time
where the time goes in v4:
time: 132 us
  Pallas kernels  130 us (98%)
    pallas_call x1, Pallas kernels, body(): pl.pallas_call(layer_kernel, out_shape=(jax.ShapeDtypeStruct((seq // 4, d...  127 us

profile of v4, /device:TPU:1, one launch (start us, length us, event | category | flops | bytes accessed | tf_op | source)
XLA Modules:
  0.0 131.7 jit_solution(2844087185799191135)
XLA Ops:
  1.3 127.0 %layer.1 = (bf16[128,2560]{1,0:T(8,128)(2,1)}, bf16[32,4,320,128]{3,2,1,0:T(8,128)(2,1)}, s32[4]{0:T(128)}) custom-call(s32[1]{0:T(128)S(6)} %copy.15.length_ref, s32[128]{0:T(128)} %slot_ref.1, bf16[512,2560]{1,0:T(8,128)(2,1)} %tok_hbm.1, s32[1,128]{1,0:T(1,128)} %bitcast.5, f32[2560]{0:T(1024)} %attn_gain_ref.1, f32[2560]{0:T(1024)} %ffn_gain_ref.1, ...), custom_call_target="tpu_custom_call" | custom-call | tf_op jit(solution)/shard_map/layer/pallas_call | solution.py:638
  128.3 0.0 copy-start
  128.3 2.6 %pick.1 = bf16[4,320,128]{2,1,0:T(8,128)(2,1)} custom-call(s32[4]{0:T(128)} %get-tuple-element.6.idx_ref, bf16[128,320,128]{2,1,0:T(8,128)(2,1)} %bitcast.3), custom_call_target="tpu_custom_call" | custom-call | tf_op jit(solution)/shard_map/pick/pallas_call | solution.py:708
  130.9 0.0 copy-done
  130.9 0.8 copy.16
Async XLA Ops:
  128.3 2.6 %copy-start = (bf16[128,2560]{1,0:T(8,128)(2,1)S(1)}, bf16[128,2560]{1,0:T(8,128)(2,1)}, u32[]{:S(2)}) copy-start(bf16[128,2560]{1,0:T(8,128)(2,1)} %get-tuple-element.10) | copy-start | bytes 1966084
